TPU v7x, 32 devices: a whole 2x2x4 slice. The times are simulated.
32 devices in a mesh: group: 2 (over x), ccd: 16 (over z, y, core).
Axes of the slice: x: 2, y: 2, z: 4, core: 2. Of those that a mesh axis runs over, the one named last changes fastest.
Arguments:
- images: float32 [4, 4096, 512], P(None, ('group', 'ccd')), parts along dimension 1, may hold values from -6 to 6
- basis_taps: float32 [2, 9, 11], replicated, may hold values from -1.75 to 1.75
- psf_coef: float32 [4, 10, 9, 3], P(None, 'group'), parts along dimension 1, may hold values from -3 to 3
- affine: float32 [4, 10, 2, 2], P(None, 'group'), parts along dimension 1, may hold values from -0.5 to 0.5
- visit_weight: bfloat16 [4, 10], P(None, 'group'), parts along dimension 1, may hold values from 0.25 to 4
- block_patch: int32 [32, 16, 1], P(('group', 'ccd')), parts along dimension 0, may hold values from 0 to 15; in each aligned block of 16 rows (0 to 15, 16 to 31, ..., all dimensions but the last counted through in order) at most 2 rows name the same one
- block_slot: int32 [32, 16], P(('group', 'ccd')), parts along dimension 0, may hold values from 0 to 15
- patch_owner: int32 [32], P('group'), parts along dimension 0, may hold values from 0 to 15, each once
Outputs:
- coadd: float32 [32, 512, 512], P(('group', 'ccd')), parts along dimension 0
There are 2 independent parts, one for each index of `group`. A program takes and returns all parts, laid end to end along the dimension named above; an argument that names none is the same for every part. Nothing has to cross between parts.
Inputs may be any that keep to these rules, and one draw needn't show every extreme that they name: `block_patch`: among the 16 blocks of one band no patch is named more than 2 times, and in every draw some band names some patch exactly 2 times. `patch_owner`: each device index along ccd owns exactly one patch.
All inputs are finite; a program needn't handle non-finite values.
Results may differ from a plain program's by a relative error of at most 0.0029.
Values may be sent and summed in bfloat16 or wider, within the bound.
A program may use at most 64 MiB of HBM per device.

v0:
```python
import functools

import jax
import jax.numpy as jnp
from jax import lax
from jax.experimental import pallas as pl
from jax.experimental.pallas import tpu as pltpu
from jax.sharding import PartitionSpec as P

V = 4
BLOCK = 128
BLKC = 4
SPLIT = 4
TAPS = 11
NBASIS = 9
PSIDE = 4
HALF = TAPS // 2
REACH = 3
RIM = HALF + REACH
ROWS_IN = BLOCK + 2 * RIM
ROWS_MID = BLOCK + 8
WIDTH = BLKC * BLOCK
HEIGHT = SPLIT * BLOCK
LEFT = BLOCK // 2
STEPS = 2 * REACH + 1


def lanczos(offset):
    inside = jnp.abs(offset) < 3.0
    return jnp.where(inside, jnp.sinc(offset) * jnp.sinc(offset / 3.0), 0.0)


def split(values):
    high = values.astype(jnp.bfloat16)
    return high, (values - high.astype(jnp.float32)).astype(jnp.bfloat16)


def dot(left, right):
    return jnp.dot(left, right, preferred_element_type=jnp.float32)


def band_kernel(
    target_ref,
    top_ref,
    above_ref,
    image_ref,
    below_ref,
    col_taps_ref,
    row_taps_ref,
    row_index_ref,
    coef_ref,
    row_weight_ref,
    col_weight_ref,
    send_ref,
    col_high,
    col_low,
    row_kernel,
    wide,
    terms_high,
    terms_low,
    mid,
):
    visit = pl.program_id(0)
    top_row = top_ref[0]
    region_low = top_ref[1]
    region_high = top_ref[2]

    @pl.when(visit == 0)
    def _():
        send_ref[...] = jnp.zeros_like(send_ref)
        depth = lax.broadcasted_iota(jnp.int32, (2 * BLOCK, BLOCK), 0)
        lane = lax.broadcasted_iota(jnp.int32, (2 * BLOCK, BLOCK), 1)
        distance = depth - (LEFT - HALF) - lane
        for basis in range(NBASIS):
            cols = pl.ds(basis * BLOCK, BLOCK)
            total = jnp.zeros((2 * BLOCK, BLOCK), jnp.float32)
            for tap in range(TAPS):
                total = jnp.where(distance == tap, col_taps_ref[tap : tap + 1, cols], total)
            high, low = split(total)
            col_high[:, cols] = high
            col_low[:, cols] = low
        gap = row_index_ref[...] - lax.broadcasted_iota(
            jnp.int32, (ROWS_MID, NBASIS * ROWS_IN), 0
        )
        total = jnp.zeros(gap.shape, jnp.float32)
        for tap in range(TAPS):
            total = jnp.where(gap == tap, row_taps_ref[tap : tap + 1, :], total)
        row_kernel[...] = total
        wide[...] = jnp.zeros_like(wide)

    def inside(first, count):
        rows = first + lax.broadcasted_iota(jnp.int32, (count, 1), 0)
        return (rows >= region_low) & (rows < region_high)

    raw = jnp.concatenate([above_ref[0], image_ref[0], below_ref[0]], axis=0)
    raw = jnp.where(inside(top_row - RIM, ROWS_IN), raw, 0.0)
    wide[:, LEFT : LEFT + WIDTH] = raw
    for block in range(BLKC):
        high, low = split(wide[:, block * BLOCK : (block + 2) * BLOCK])
        term = dot(high, col_high[...]) + dot(low, col_high[...]) + dot(high, col_low[...])
        high, low = split(term)
        for basis in range(NBASIS):
            rows = pl.ds(basis * ROWS_IN, ROWS_IN)
            cols = pl.ds(block * BLOCK, BLOCK)
            terms_high[rows, cols] = high[:, basis * BLOCK : (basis + 1) * BLOCK]
            terms_low[rows, cols] = low[:, basis * BLOCK : (basis + 1) * BLOCK]

    position = (top_row - REACH + lax.broadcasted_iota(jnp.int32, (ROWS_MID, 1), 0)).astype(
        jnp.float32
    )
    row_pos = (2.0 * position + 1.0) / HEIGHT - 1.0
    column = lax.broadcasted_iota(jnp.int32, (1, WIDTH), 1).astype(jnp.float32)
    col_pos = (2.0 * column + 1.0) / WIDTH - 1.0
    kernel = row_kernel[...]
    level = kernel * (coef_ref[0, 0:1, :] + coef_ref[0, 1:2, :] * row_pos)
    slope = kernel * coef_ref[0, 2:3, :]
    level_high, level_low = split(level)
    slope_high, slope_low = split(slope)
    upper = dot(
        jnp.concatenate([level_high, slope_high, level_low, slope_low], axis=0), terms_high[...]
    )
    lower = dot(jnp.concatenate([level_high, slope_high], axis=0), terms_low[...])
    both = upper[: 2 * ROWS_MID] + upper[2 * ROWS_MID :] + lower
    matched = both[:ROWS_MID] + both[ROWS_MID:] * col_pos
    mid[...] = jnp.where(inside(top_row - REACH, ROWS_MID), matched, 0.0)

    warped = jnp.zeros((BLOCK, WIDTH), jnp.float32)
    for step in range(STEPS):
        warped = warped + row_weight_ref[0, :, step : step + 1] * mid[step : step + BLOCK, :]
    total = jnp.zeros((BLOCK, WIDTH), jnp.float32)
    for step in range(STEPS):
        offset = step - REACH
        moved = warped if offset == 0 else pltpu.roll(warped, (-offset) % WIDTH, 1)
        total = total + col_weight_ref[0, step : step + 1, :] * moved
    rounded = total.astype(jnp.bfloat16)
    for block in range(BLKC):
        send_ref[target_ref[visit * BLKC + block]] = rounded[
            :, block * BLOCK : (block + 1) * BLOCK
        ]


def gather_kernel(count, cell_ref, weight_ref, got_ref, out_ref, total, weights):
    total[...] = jnp.zeros_like(total)
    for cell in range(PSIDE * PSIDE):
        weights[cell] = 0.0

    def add(index, carry):
        cell = cell_ref[index]

        @pl.when(cell >= 0)
        def _():
            weight = weight_ref[index]
            weights[cell] = weights[cell] + weight
            total[cell] = total[cell] + weight * got_ref[index].astype(jnp.float32)

        return carry

    lax.fori_loop(0, count, add, 0)
    for cell in range(PSIDE * PSIDE):
        row, col = cell // PSIDE * BLOCK, cell % PSIDE * BLOCK
        scale = jnp.full((1, BLOCK), jnp.maximum(weights[cell], 1.0), jnp.float32)
        out_ref[0, row : row + BLOCK, col : col + BLOCK] = total[cell] / scale


def shards(
    images, basis_taps, psf_coef, affine, visit_weight, block_patch, block_slot, patch_owner
):
    band_index = lax.axis_index("ccd")
    devices = lax.axis_size("ccd")
    ends = devices - 1
    above = lax.ppermute(
        images[:, BLOCK - RIM :], "ccd", [(i, i + 1) for i in range(ends)]
    )
    below = lax.ppermute(images[:, :RIM], "ccd", [(i + 1, i) for i in range(ends)])
    shifted_band = band_index + SPLIT // 2
    ccd_index = shifted_band // SPLIT
    top_row = shifted_band % SPLIT * BLOCK
    region_shift = band_index * BLOCK - top_row
    limits = jnp.stack(
        [
            top_row,
            jnp.maximum(0, -region_shift),
            jnp.minimum(HEIGHT, devices * BLOCK - region_shift),
        ]
    ).astype(jnp.int32)

    block_count = V * BLKC
    capacity = max(2, (2 * block_count + devices - 1) // devices)
    slots = devices * capacity
    patch_ids = block_patch[0, :, 0]
    owner_match = patch_ids[:, None] == jnp.arange(patch_owner.shape[0])[None, :]
    destination = jnp.sum(jnp.where(owner_match, patch_owner[None, :], 0), axis=1)
    order = jnp.arange(block_count)
    same_owner = destination[:, None] == destination[None, :]
    rank = jnp.sum((same_owner & (order[None, :] < order[:, None])).astype(jnp.int32), axis=1)
    target = (destination * capacity + rank).astype(jnp.int32)
    hit = target[None, :] == jnp.arange(slots)[:, None]
    code = block_slot[0] * V + order // BLKC
    codes = jnp.sum(jnp.where(hit, code[None, :] + 1, 0), axis=1) - 1
    got_codes = lax.all_to_all(
        codes.reshape(devices, capacity), "ccd", split_axis=0, concat_axis=0, tiled=True
    )

    terms_here = lax.dynamic_index_in_dim(psf_coef, ccd_index, 1, keepdims=False)
    affine_here = lax.dynamic_index_in_dim(affine, ccd_index, 1, keepdims=False)
    coef = jnp.repeat(terms_here.transpose(0, 2, 1), ROWS_IN, axis=2)
    col_taps = jnp.repeat(basis_taps[1].T, BLOCK, axis=1)
    row_taps = jnp.repeat(basis_taps[0].T, ROWS_IN, axis=1)
    row_index = (jnp.arange(NBASIS * ROWS_IN, dtype=jnp.int32) % ROWS_IN)[None]
    steps = jnp.arange(STEPS) - REACH
    rows = (top_row + jnp.arange(BLOCK)).astype(jnp.float32)
    row_shift = affine_here[:, 0, 0:1] + affine_here[:, 0, 1:2] * (
        (rows - (HEIGHT - 1) / 2.0) / HEIGHT
    )
    row_weight = lanczos(row_shift[:, :, None] - steps.astype(jnp.float32))
    cols = jnp.arange(WIDTH)
    col_shift = affine_here[:, 1, 0:1] + affine_here[:, 1, 1:2] * (
        (cols.astype(jnp.float32) - (WIDTH - 1) / 2.0) / WIDTH
    )
    reached = cols[None, :] + steps[:, None]
    col_weight = jnp.where(
        (reached >= 0) & (reached < WIDTH),
        lanczos(col_shift[:, None, :] - steps.astype(jnp.float32)[:, None]),
        0.0,
    )

    def per_visit(shape):
        return pl.BlockSpec((1,) + shape[1:], lambda v, *_: (v, 0, 0))

    def whole(shape):
        return pl.BlockSpec(shape, lambda v, *_: (0,) * len(shape))

    out_shape = (slots, BLOCK, BLOCK)
    send = pl.pallas_call(
        band_kernel,
        out_shape=jax.ShapeDtypeStruct(out_shape, jnp.bfloat16),
        grid_spec=pltpu.PrefetchScalarGridSpec(
            num_scalar_prefetch=2,
            grid=(V,),
            in_specs=[
                per_visit(above.shape),
                per_visit(images.shape),
                per_visit(below.shape),
                whole(col_taps.shape),
                whole(row_taps.shape),
                whole(row_index.shape),
                per_visit(coef.shape),
                per_visit(row_weight.shape),
                per_visit(col_weight.shape),
            ],
            out_specs=whole(out_shape),
            scratch_shapes=[
                pltpu.VMEM((2 * BLOCK, NBASIS * BLOCK), jnp.bfloat16),
                pltpu.VMEM((2 * BLOCK, NBASIS * BLOCK), jnp.bfloat16),
                pltpu.VMEM((ROWS_MID, NBASIS * ROWS_IN), jnp.float32),
                pltpu.VMEM((ROWS_IN, WIDTH + BLOCK), jnp.float32),
                pltpu.VMEM((NBASIS * ROWS_IN, WIDTH), jnp.bfloat16),
                pltpu.VMEM((NBASIS * ROWS_IN, WIDTH), jnp.bfloat16),
                pltpu.VMEM((ROWS_MID, WIDTH), jnp.float32),
            ],
        ),
        compiler_params=pltpu.CompilerParams(dimension_semantics=("arbitrary",)),
    )(
        target,
        limits,
        above,
        images,
        below,
        col_taps,
        row_taps,
        row_index,
        coef,
        row_weight,
        col_weight,
    )
    got = lax.all_to_all(
        send.reshape(devices, capacity, BLOCK, BLOCK),
        "ccd",
        split_axis=0,
        concat_axis=0,
        tiled=True,
    ).reshape(out_shape)
    source_ccd = (jnp.arange(devices) + SPLIT // 2) // SPLIT
    by_source = visit_weight.astype(jnp.float32).T[source_ccd]
    used = got_codes >= 0
    cell = jnp.where(used, got_codes // V, -1).reshape(slots)
    which = jnp.arange(V)[None, None, :] == (got_codes % V)[:, :, None]
    weight = jnp.sum(jnp.where(which, by_source[:, None, :], 0.0), axis=2).reshape(slots)
    size = PSIDE * BLOCK
    return pl.pallas_call(
        functools.partial(gather_kernel, slots),
        out_shape=jax.ShapeDtypeStruct((1, size, size), jnp.float32),
        in_specs=[
            pl.BlockSpec(memory_space=pltpu.SMEM),
            pl.BlockSpec(memory_space=pltpu.SMEM),
            pl.BlockSpec(memory_space=pltpu.VMEM),
        ],
        out_specs=pl.BlockSpec(memory_space=pltpu.VMEM),
        scratch_shapes=[
            pltpu.VMEM((PSIDE * PSIDE, BLOCK, BLOCK), jnp.float32),
            pltpu.SMEM((PSIDE * PSIDE,), jnp.float32),
        ],
    )(cell, weight, got)


def solution(mesh):
    placed = (
        P(None, ("group", "ccd"), None),
        P(),
        P(None, "group", None, None),
        P(None, "group", None, None),
        P(None, "group"),
        P(("group", "ccd"), None, None),
        P(("group", "ccd"), None),
        P("group"),
    )
    return jax.shard_map(
        shards,
        mesh=mesh,
        in_specs=placed,
        out_specs=P(("group", "ccd"), None, None),
        check_vma=False,
    )
```

profile of v0, /device:TPU:11, one launch (start us, length us, event | category | flops | bytes accessed | tf_op | source)
XLA Modules:
  0.0 76.4 jit_solution(18373138487819593213)
XLA Ops:
  0.0 0.0 copy-start
  0.0 0.9 %fusion.101 = (f32[4,8,512]{2,1,0:T(8,128)S(1)}, f32[4,8,512]{2,1,0:T(8,128)S(1)}) fusion(f32[4,128,512]{2,1,0:T(8,128)} %image_ref.1), kind=kLoop, calls=%fused_computation.173 | loop fusion | bytes 262144 | tf_op jit(solution)/shard_map/slice | solution.py:174
  0.9 3.7 %collective-permute-start = (f32[4,8,512]{2,1,0:T(8,128)S(1)}, f32[4,8,512]{2,1,0:T(8,128)S(1)}, u32[]{:S(2)}, u32[]{:S(2)}) collective-permute-start(f32[4,8,512]{2,1,0:T(8,128)S(1)} %get-tuple-element.8), channel_id=1, source_target_pairs={{0,1},{1,2},{2,3},{3,4},{4,5},{5,6},{6,7},{7,8},{8,9},{9,10},{10,1... | collective-permute-start | bytes 196616 | tf_op jit(solution)/shard_map/ppermute | solution.py:171
  4.6 0.0 copy-start.8
  4.6 0.0 copy-start.9
  4.6 1.9 %collective-permute-start.1 = (f32[4,8,512]{2,1,0:T(8,128)S(1)}, f32[4,8,512]{2,1,0:T(8,128)S(1)}, u32[]{:S(2)}, u32[]{:S(2)}) collective-permute-start(f32[4,8,512]{2,1,0:T(8,128)S(1)} %get-tuple-element.6), channel_id=1, source_target_pairs={{1,0},{2,1},{3,2},{4,3},{5,4},{6,5},{7,6},{8,7},{9,8},{10,9},{11,1... | collective-permute-start | bytes 196616 | tf_op jit(solution)/shard_map/ppermute | solution.py:174
  6.6 0.0 copy-done.8
  6.6 0.0 copy-done.9
  6.6 0.2 select_reduce_fusion.1
  6.8 0.2 convert_reduce_fusion
  6.9 0.0 copy-start.10
  7.0 0.6 copy-done.10
  7.6 0.0 copy-start.7
  7.6 0.6 copy-done.7
  8.2 0.1 select_reduce_fusion
  8.3 0.7 sub.84
  9.0 6.5 %all-to-all-start = ((s32[16,1,2]{2,1,0:T(1,128)}), s32[16,1,2]{2,1,0:T(1,128)S(1)}, u32[]{:S(2)}, u32[]{:S(2)}) async-start(s32[16,1,2]{2,1,0:T(1,128)} %bitcast.2), calls=%async_computation | async-start | bytes 16384 | tf_op jit(solution)/shard_map/all_to_all | solution.py:200
  15.5 0.6 and_select_fusion.row_index_ref
  16.1 0.0 copy-start.5
  16.1 0.7 copy-done.5
  16.8 0.1 constant_dynamic-slice_fusion
  16.9 0.1 copy.57
  17.0 0.0 copy-done
  17.0 0.1 broadcast_in_dim.99
  17.1 0.1 reshape.307
  17.3 0.7 copy.58.coef_ref
  17.9 0.0 copy-start.4
  17.9 0.1 fusion.93
  18.0 0.6 copy-done.4
  18.6 0.1 copy.61
  18.7 0.1 broadcast_in_dim.97
  18.8 0.6 copy.63
  19.5 0.1 copy.62
  19.6 0.1 broadcast_in_dim.98
  19.7 0.7 reshape.306.row_taps_ref
  20.4 0.1 multiply_add_fusion.5
  20.5 1.4 %fusion.16.row_weight_ref = f32[4,128,7]{2,1,0:T(8,128)} fusion(f32[7]{0:T(128)S(1)} %fusion.100, f32[4,128]{1,0:T(4,128)S(1)} %multiply_add_fusion.5), kind=kLoop, calls=%fused_computation.27 | loop fusion | flops 254464 | bytes 16412 | tf_op jit(solution)/shard_map/jit(_where)/select_n | solution.py:30
  21.9 0.1 multiply_add_fusion.4
  21.9 0.9 %fusion.90.col_weight_ref = f32[4,7,512]{2,1,0:T(8,128)} fusion(f32[7]{0:T(128)S(1)} %fusion.100, f32[4,512]{1,0:T(4,128)S(1)} %multiply_add_fusion.4, pred[7,512]{1,0:T(8,128)(4,1)S(1)} %fusion.93), kind=kLoop, calls=%fused_computation.119 | loop fusion | flops 1032192 | bytes 69148 | tf_op jit(solution)/shard_map/jit(_where)/select_n | solution.py:221
  22.8 0.6 pad_add_fusion.top_ref
  23.4 0.0 collective-permute-done.above_ref
  23.4 0.0 copy-start.2
  23.4 0.0 collective-permute-done.1.below_ref
  23.4 0.0 copy-start.3
  23.4 0.6 copy-done.2
  24.0 0.0 copy-done.3
  24.0 17.5 %shard_map.82 = bf16[32,128,128]{2,1,0:T(8,128)(2,1)} custom-call(s32[16]{0:T(128)} %copy-done.7, s32[3]{0:T(128)} %pad_add_fusion.top_ref, f32[4,8,512]{2,1,0:T(8,128)} %copy-done.2, f32[4,128,512]{2,1,0:T(8,128)} %image_ref.1, f32[4,8,512]{2,1,0:T(8,128)} %copy-done.3, f32[11,1152]{1,0:T(8,128)} %bitcast.44, f32[11,1296]{1,0:T(8,128)} %reshape.306.row_taps_ref, ...), custom_call_target="tpu_custom_call" | custom-call | tf_op jit(solution)/shard_map/pallas_call | solution.py:234
  41.5 0.0 all-to-all-done
  41.5 0.0 copy-start.6
  41.6 6.0 %all-to-all-start.1 = ((bf16[16,2,128,128]{3,2,1,0:T(8,128)(2,1)}), bf16[16,2,128,128]{3,2,1,0:T(8,128)(2,1)S(1)}, u32[]{:S(2)}, u32[]{:S(2)}) async-start(bf16[16,2,128,128]{3,2,1,0:T(8,128)(2,1)} %bitcast.41), calls=%async_computation.1 | async-start | bytes 2097152 | tf_op jit(solution)/shard_map/all_to_all | solution.py:276
  47.6 0.0 copy-done.6
  47.6 0.1 copy.50
  47.7 0.6 gather_fusion
  48.3 0.1 copy.51
  48.4 0.1 copy.49
  48.5 0.1 copy.52
  48.6 0.7 reshape.304.weight_ref
  49.2 0.5 broadcast.398
  49.7 0.6 reduce.3
  50.3 0.1 all_to_all.12
  50.4 0.5 compare_select_fusion.3.cell_ref
  51.0 21.5 %all-to-all-done.1 = bf16[16,2,128,128]{3,2,1,0:T(8,128)(2,1)S(1)} async-done(((bf16[16,2,128,128]{3,2,1,0:T(8,128)(2,1)}), bf16[16,2,128,128]{3,2,1,0:T(8,128)(2,1)S(1)}, u32[]{:S(2)}, u32[]{:S(2)}) %all-to-all-start.1) | async-done | bytes 1048608 | tf_op jit(solution)/shard_map/all_to_all | solution.py:276
  72.5 1.0 %copy-done.1 = bf16[16,2,128,128]{3,2,1,0:T(8,128)(2,1)} copy-done((bf16[16,2,128,128]{3,2,1,0:T(8,128)(2,1)}, bf16[16,2,128,128]{3,2,1,0:T(8,128)(2,1)S(1)}, u32[]{:S(2)}) %copy-start.1) | copy-done | bytes 1048600
  73.5 2.9 %shard_map.83 = f32[1,512,512]{2,1,0:T(8,128)} custom-call(s32[32]{0:T(128)} %compare_select_fusion.3.cell_ref, f32[32]{0:T(128)} %reshape.304.weight_ref, bf16[32,128,128]{2,1,0:T(8,128)(2,1)} %bitcast.42), custom_call_target="tpu_custom_call" | custom-call | tf_op jit(solution)/shard_map/pallas_call | solution.py:290
  (17 shorter events, 0.1 us)
Async XLA Ops:
  0.0 17.0 %copy-start = (f32[4,5,9,3]{2,0,3,1:T(4,128)S(1)}, f32[4,5,9,3]{2,0,3,1:T(4,128)}, u32[]{:S(2)}) copy-start(f32[4,5,9,3]{2,0,3,1:T(4,128)} %param.12) | copy-start | bytes 6484
  0.9 22.5 %collective-permute-start = (f32[4,8,512]{2,1,0:T(8,128)S(1)}, f32[4,8,512]{2,1,0:T(8,128)S(1)}, u32[]{:S(2)}, u32[]{:S(2)}) collective-permute-start(f32[4,8,512]{2,1,0:T(8,128)S(1)} %get-tuple-element.8), channel_id=1, source_target_pairs={{0,1},{1,2},{2,3},{3,4},{4,5},{5,6},{6,7},{7,8},{8,9},{9,10},{10,1... | collective-permute-start | bytes 196616 | tf_op jit(solution)/shard_map/ppermute | solution.py:171
  4.6 2.0 %copy-start.8 = (s32[16]{0:T(128)S(1)}, s32[16]{0:T(128)}, u32[]{:S(2)}) copy-start(s32[16]{0:T(128)} %param.17) | copy-start | bytes 196
  4.6 2.0 %copy-start.9 = (s32[1,16,1]{1,2,0:T(1,128)S(1)}, s32[1,16,1]{1,2,0:T(1,128)}, u32[]{:S(2)}) copy-start(s32[1,16,1]{1,2,0:T(1,128)} %param.15) | copy-start | bytes 196
  4.6 18.8 %collective-permute-start.1 = (f32[4,8,512]{2,1,0:T(8,128)S(1)}, f32[4,8,512]{2,1,0:T(8,128)S(1)}, u32[]{:S(2)}, u32[]{:S(2)}) collective-permute-start(f32[4,8,512]{2,1,0:T(8,128)S(1)} %get-tuple-element.6), channel_id=1, source_target_pairs={{1,0},{2,1},{3,2},{4,3},{5,4},{6,5},{7,6},{8,7},{9,8},{10,9},{11,1... | collective-permute-start | bytes 196616 | tf_op jit(solution)/shard_map/ppermute | solution.py:174
  6.9 0.7 copy-start.10
  7.6 0.6 copy-start.7
  9.0 32.6 %all-to-all-start = ((s32[16,1,2]{2,1,0:T(1,128)}), s32[16,1,2]{2,1,0:T(1,128)S(1)}, u32[]{:S(2)}, u32[]{:S(2)}) async-start(s32[16,1,2]{2,1,0:T(1,128)} %bitcast.2), calls=%async_computation | async-start | bytes 16384 | tf_op jit(solution)/shard_map/all_to_all | solution.py:200
  16.1 0.7 copy-start.5
  17.9 0.7 copy-start.4
  23.4 0.6 copy-start.2
  23.4 0.6 copy-start.3
  41.5 6.0 %copy-start.6 = (bf16[4,5]{1,0:T(4,128)(2,1)S(1)}, bf16[4,5]{1,0:T(4,128)(2,1)}, u32[]{:S(2)}) copy-start(bf16[4,5]{1,0:T(4,128)(2,1)} %param.14) | copy-start | bytes 124
  41.6 31.0 %all-to-all-start.1 = ((bf16[16,2,128,128]{3,2,1,0:T(8,128)(2,1)}), bf16[16,2,128,128]{3,2,1,0:T(8,128)(2,1)S(1)}, u32[]{:S(2)}, u32[]{:S(2)}) async-start(bf16[16,2,128,128]{3,2,1,0:T(8,128)(2,1)} %bitcast.41), calls=%async_computation.1 | async-start | bytes 2097152 | tf_op jit(solution)/shard_map/all_to_all | solution.py:276
  72.5 1.0 %copy-start.1 = (bf16[16,2,128,128]{3,2,1,0:T(8,128)(2,1)}, bf16[16,2,128,128]{3,2,1,0:T(8,128)(2,1)S(1)}, u32[]{:S(2)}) copy-start(bf16[16,2,128,128]{3,2,1,0:T(8,128)(2,1)S(1)} %all-to-all-done.1) | copy-start | bytes 3145732
where the time goes:
time: 76.9 us; the launch traced here: 76.4 us
  waiting for transfers between devices  21.5 us (28%)
  Pallas kernels  20.4 us (27%)
  starting transfers between devices  18.2 us (24%)
  local copies, waits for them, and re-layouts  10.7 us (14%)
  other arithmetic  5.34 us (7%)
    all_to_all x1, waiting for transfers between devices, shards(): lax.all_to_all(send.reshape(devices, capacity, BLOCK, BLOCK), 'ccd', spli...  21.5 us
    pallas_call x1, Pallas kernels, shards(): pl.pallas_call(band_kernel, out_shape=jax.ShapeDtypeStruct(out_shape, jnp...  17.5 us
    all_to_all x1, starting transfers between devices, shards(): lax.all_to_all(codes.reshape(devices, capacity), 'ccd', split_axis=0, con...  6.51 us
    all_to_all x1, starting transfers between devices, shards(): lax.all_to_all(send.reshape(devices, capacity, BLOCK, BLOCK), 'ccd', spli...  6.03 us
    unnamed x25, local copies, waits for them, and re-layouts  4.9 us
    ppermute x1, starting transfers between devices, shards(): lax.ppermute(images[:, BLOCK - RIM:], 'ccd', [(i, i + 1) for i in range(e...  3.71 us
    pallas_call x1, Pallas kernels, shards(): pl.pallas_call(functools.partial(gather_kernel, slots), out_shape=jax.Sha...  2.93 us
    ppermute x1, starting transfers between devices, shards(): lax.ppermute(images[:, :RIM], 'ccd', [(i + 1, i) for i in range(ends)])  1.92 us
  transfers between devices with their start and end apart: 4, of which 1 were waited for; matrix products, arithmetic and copies ran while one was open for 14% of the time, Pallas kernels for 23%

commit v1 on v0

v1 whole, which is shorter than its diff:
```python
import functools

import jax
import jax.numpy as jnp
from jax import lax
from jax.experimental import pallas as pl
from jax.experimental.pallas import tpu as pltpu
from jax.sharding import PartitionSpec as P

V = 4
BLOCK = 128
BLKC = 4
SPLIT = 4
TAPS = 11
NBASIS = 9
PSIDE = 4
HALF = TAPS // 2
REACH = 3
RIM = HALF + REACH
ROWS_IN = BLOCK + 2 * RIM
ROWS_MID = BLOCK + 8
WIDTH = BLKC * BLOCK
HEIGHT = SPLIT * BLOCK
LEFT = BLOCK // 2
STEPS = 2 * REACH + 1


def sinc(values):
    angle = jnp.pi * values
    zero = values == 0.0
    return jnp.where(zero, 1.0, jnp.sin(angle) / jnp.where(zero, 1.0, angle))


def lanczos(offset):
    inside = jnp.abs(offset) < 3.0
    return jnp.where(inside, sinc(offset) * sinc(offset / 3.0), 0.0)


def outward(count):
    return sorted(range(1, count), key=lambda step: abs(step - count // 2))


def meet(me, count):
    barrier = pltpu.get_barrier_semaphore()
    for step in range(1, count):
        pl.semaphore_signal(
            barrier,
            inc=1,
            device_id={"ccd": lax.rem(me + step, count)},
            device_id_type=pl.DeviceIdType.MESH,
        )
    pl.semaphore_wait(barrier, count - 1)


def rim_kernel(count, image_ref, meta_ref, above_ref, below_ref, metas_ref, sent, received, rims, own):
    me = lax.axis_index("ccd")
    meet(me, count)

    def remote(source, target, send, receive, step):
        return pltpu.make_async_remote_copy(
            src_ref=source,
            dst_ref=target,
            send_sem=send,
            recv_sem=receive,
            device_id={"ccd": lax.rem(me + step, count)},
            device_id_type=pl.DeviceIdType.MESH,
        )

    copies = [
        remote(image_ref.at[:, pl.ds(BLOCK - RIM, RIM)], above_ref, rims.at[0], rims.at[1], 1),
        remote(image_ref.at[:, pl.ds(0, RIM)], below_ref, rims.at[2], rims.at[3], count - 1),
    ]
    for step in outward(count):
        copies.append(
            remote(meta_ref, metas_ref.at[me], sent.at[step], received.at[step], step)
        )
    for copy in copies:
        copy.start()
    local = pltpu.make_async_copy(meta_ref, metas_ref.at[me], own)
    local.start()
    local.wait()
    for copy in copies:
        copy.wait()


def trade_kernel(count, send_ref, got_ref, sent, received, own):
    me = lax.axis_index("ccd")
    meet(me, count)
    copies = []
    for step in outward(count):
        peer = lax.rem(me + step, count)
        copies.append(
            pltpu.make_async_remote_copy(
                src_ref=send_ref.at[peer],
                dst_ref=got_ref.at[me],
                send_sem=sent.at[step],
                recv_sem=received.at[step],
                device_id={"ccd": peer},
                device_id_type=pl.DeviceIdType.MESH,
            )
        )
    for copy in copies:
        copy.start()
    local = pltpu.make_async_copy(send_ref.at[me], got_ref.at[me], own)
    local.start()
    local.wait()
    for copy in copies:
        copy.wait()


def split(values):
    high = values.astype(jnp.bfloat16)
    return high, (values - high.astype(jnp.float32)).astype(jnp.bfloat16)


def dot(left, right):
    return jnp.dot(left, right, preferred_element_type=jnp.float32)


def band_kernel(
    devices,
    capacity,
    patch_ref,
    owner_ref,
    taps_ref,
    coef_ref,
    affine_ref,
    above_ref,
    image_ref,
    below_ref,
    send_ref,
    col_high,
    col_low,
    row_kernel,
    wide,
    terms_high,
    terms_low,
    mid,
    target,
    filled,
):
    visit = pl.program_id(0)
    band = lax.axis_index("ccd")
    shifted = band + SPLIT // 2
    ccd = shifted // SPLIT
    top_row = shifted % SPLIT * BLOCK
    region_shift = band * BLOCK - top_row
    region_low = jnp.maximum(0, -region_shift)
    region_high = jnp.minimum(HEIGHT, devices * BLOCK - region_shift)
    ccds = coef_ref.shape[0] // (V * NBASIS * 3)
    place = visit * ccds + ccd
    wide_lane = lax.broadcasted_iota(jnp.int32, (1, NBASIS * ROWS_IN), 1)

    def by_basis(value):
        total = jnp.full((1, NBASIS * ROWS_IN), value(0), jnp.float32)
        for basis in range(1, NBASIS):
            total = jnp.where(wide_lane >= basis * ROWS_IN, value(basis), total)
        return total

    @pl.when(visit == 0)
    def _():
        send_ref[...] = jnp.zeros_like(send_ref)
        for device in range(devices):
            filled[device] = 0
        for block in range(V * BLKC):
            device = owner_ref[patch_ref[block]]
            target[block] = device * capacity + filled[device]
            filled[device] = filled[device] + 1
        depth = lax.broadcasted_iota(jnp.int32, (2 * BLOCK, BLOCK), 0)
        lane = lax.broadcasted_iota(jnp.int32, (2 * BLOCK, BLOCK), 1)
        distance = depth - (LEFT - HALF) - lane
        for basis in range(NBASIS):
            cols = pl.ds(basis * BLOCK, BLOCK)
            total = jnp.zeros((2 * BLOCK, BLOCK), jnp.float32)
            for tap in range(TAPS):
                total = jnp.where(
                    distance == tap, taps_ref[(NBASIS + basis) * TAPS + tap], total
                )
            high, low = split(total)
            col_high[:, cols] = high
            col_low[:, cols] = low
        start = jnp.zeros((1, NBASIS * ROWS_IN), jnp.int32)
        for basis in range(1, NBASIS):
            start = jnp.where(wide_lane >= basis * ROWS_IN, basis * ROWS_IN, start)
        gap = (wide_lane - start) - lax.broadcasted_iota(
            jnp.int32, (ROWS_MID, NBASIS * ROWS_IN), 0
        )
        total = jnp.zeros(gap.shape, jnp.float32)
        for tap in range(TAPS):
            total = jnp.where(
                gap == tap, by_basis(lambda basis: taps_ref[basis * TAPS + tap]), total
            )
        row_kernel[...] = total
        wide[...] = jnp.zeros_like(wide)

    def inside(first, count):
        rows = first + lax.broadcasted_iota(jnp.int32, (count, 1), 0)
        return (rows >= region_low) & (rows < region_high)

    raw = jnp.concatenate([above_ref[0], image_ref[0], below_ref[0]], axis=0)
    raw = jnp.where(inside(top_row - RIM, ROWS_IN), raw, 0.0)
    wide[:, LEFT : LEFT + WIDTH] = raw
    for block in range(BLKC):
        high, low = split(wide[:, block * BLOCK : (block + 2) * BLOCK])
        term = dot(high, col_high[...]) + dot(low, col_high[...]) + dot(high, col_low[...])
        high, low = split(term)
        for basis in range(NBASIS):
            rows = pl.ds(basis * ROWS_IN, ROWS_IN)
            cols = pl.ds(block * BLOCK, BLOCK)
            terms_high[rows, cols] = high[:, basis * BLOCK : (basis + 1) * BLOCK]
            terms_low[rows, cols] = low[:, basis * BLOCK : (basis + 1) * BLOCK]

    position = (top_row - REACH + lax.broadcasted_iota(jnp.int32, (ROWS_MID, 1), 0)).astype(
        jnp.float32
    )
    row_pos = (2.0 * position + 1.0) / HEIGHT - 1.0
    column = lax.broadcasted_iota(jnp.int32, (1, WIDTH), 1).astype(jnp.float32)
    col_pos = (2.0 * column + 1.0) / WIDTH - 1.0
    kernel = row_kernel[...]
    constant, by_row, by_column = (
        by_basis(lambda basis: coef_ref[(place * NBASIS + basis) * 3 + part]) for part in range(3)
    )
    level = kernel * (constant + by_row * row_pos)
    slope = kernel * by_column
    level_high, level_low = split(level)
    slope_high, slope_low = split(slope)
    upper = dot(
        jnp.concatenate([level_high, slope_high, level_low, slope_low], axis=0), terms_high[...]
    )
    lower = dot(jnp.concatenate([level_high, slope_high], axis=0), terms_low[...])
    both = upper[: 2 * ROWS_MID] + upper[2 * ROWS_MID :] + lower
    matched = both[:ROWS_MID] + both[ROWS_MID:] * col_pos
    mid[...] = jnp.where(inside(top_row - REACH, ROWS_MID), matched, 0.0)

    own_rows = (top_row + lax.broadcasted_iota(jnp.int32, (BLOCK, 1), 0)).astype(jnp.float32)
    row_shift = affine_ref[place * 4] + affine_ref[place * 4 + 1] * (
        (own_rows - (HEIGHT - 1) / 2.0) / HEIGHT
    )
    row_step = lax.broadcasted_iota(jnp.int32, (BLOCK, BLOCK), 1) - REACH
    row_weight = lanczos(row_shift - row_step.astype(jnp.float32))
    col_shift = affine_ref[place * 4 + 2] + affine_ref[place * 4 + 3] * (
        (column - (WIDTH - 1) / 2.0) / WIDTH
    )
    col_step = lax.broadcasted_iota(jnp.int32, (8, WIDTH), 0) - REACH
    reached = lax.broadcasted_iota(jnp.int32, (8, WIDTH), 1) + col_step
    col_weight = jnp.where(
        (reached >= 0) & (reached < WIDTH),
        lanczos(col_shift - col_step.astype(jnp.float32)),
        0.0,
    )
    warped = jnp.zeros((BLOCK, WIDTH), jnp.float32)
    for step in range(STEPS):
        warped = warped + row_weight[:, step : step + 1] * mid[step : step + BLOCK, :]
    total = jnp.zeros((BLOCK, WIDTH), jnp.float32)
    for step in range(STEPS):
        offset = step - REACH
        moved = warped if offset == 0 else pltpu.roll(warped, (-offset) % WIDTH, 1)
        total = total + col_weight[step : step + 1, :] * moved
    rounded = total.astype(jnp.bfloat16)
    for block in range(BLKC):
        send_ref[target[visit * BLKC + block]] = rounded[
            :, block * BLOCK : (block + 1) * BLOCK
        ]


def gather_kernel(devices, capacity, meta_ref, owner_ref, weight_ref, got_ref, out_ref, total, weights):
    me = lax.axis_index("ccd")
    total[...] = jnp.zeros_like(total)
    for cell in range(PSIDE * PSIDE):
        weights[cell] = 0.0
    patch = jnp.int32(0)
    for candidate in range(owner_ref.shape[0]):
        patch = jnp.where(owner_ref[candidate] == me, candidate, patch)
    ccds = weight_ref.shape[0] // V
    count = V * BLKC

    def add(source, carry):
        ccd = (source + SPLIT // 2) // SPLIT
        taken = source * capacity
        for block in range(count):
            mine = meta_ref[source, 0, block] == patch

            @pl.when(mine)
            def _(taken=taken, block=block):
                cell = meta_ref[source, 0, count + block]
                weight = weight_ref[block // BLKC * ccds + ccd]
                weights[cell] = weights[cell] + weight
                total[cell] = total[cell] + weight * got_ref[taken].astype(jnp.float32)

            taken = taken + mine.astype(jnp.int32)
        return carry

    lax.fori_loop(0, devices, add, 0)
    for cell in range(PSIDE * PSIDE):
        row, col = cell // PSIDE * BLOCK, cell % PSIDE * BLOCK
        scale = jnp.full((1, BLOCK), jnp.maximum(weights[cell], 1.0), jnp.float32)
        out_ref[0, row : row + BLOCK, col : col + BLOCK] = total[cell] / scale


def shards(
    images, basis_taps, psf_coef, affine, visit_weight, block_patch, block_slot, patch_owner
):
    devices = lax.axis_size("ccd")
    block_count = V * BLKC
    capacity = max(2, (2 * block_count + devices - 1) // devices)
    slots = devices * capacity
    anywhere = pl.BlockSpec(memory_space=pl.ANY)
    scalars = pl.BlockSpec(memory_space=pltpu.SMEM)
    vector = pl.BlockSpec(memory_space=pltpu.VMEM)
    lanes = -(-2 * block_count // BLOCK) * BLOCK
    meta = jnp.pad(
        jnp.concatenate([block_patch[0, :, 0], block_slot[0]]), (0, lanes - 2 * block_count)
    )[None]
    rim_shape = jax.ShapeDtypeStruct((V, RIM, WIDTH), jnp.float32)
    above, below, metas = pl.pallas_call(
        functools.partial(rim_kernel, devices),
        out_shape=(rim_shape, rim_shape, jax.ShapeDtypeStruct((devices, 1, lanes), jnp.int32)),
        in_specs=[anywhere, vector],
        out_specs=(anywhere, anywhere, vector),
        scratch_shapes=[
            pltpu.SemaphoreType.DMA((devices,)),
            pltpu.SemaphoreType.DMA((devices,)),
            pltpu.SemaphoreType.DMA((4,)),
            pltpu.SemaphoreType.DMA,
        ],
        compiler_params=pltpu.CompilerParams(collective_id=1, has_side_effects=True),
    )(images, meta)

    def per_visit(shape):
        return pl.BlockSpec((1,) + shape[1:], lambda v: (v, 0, 0))

    out_shape = (slots, BLOCK, BLOCK)
    send = pl.pallas_call(
        functools.partial(band_kernel, devices, capacity),
        out_shape=jax.ShapeDtypeStruct(out_shape, jnp.bfloat16),
        grid=(V,),
        in_specs=[scalars] * 5
        + [per_visit(above.shape), per_visit(images.shape), per_visit(below.shape)],
        out_specs=pl.BlockSpec(out_shape, lambda v: (0, 0, 0)),
        scratch_shapes=[
            pltpu.VMEM((2 * BLOCK, NBASIS * BLOCK), jnp.bfloat16),
            pltpu.VMEM((2 * BLOCK, NBASIS * BLOCK), jnp.bfloat16),
            pltpu.VMEM((ROWS_MID, NBASIS * ROWS_IN), jnp.float32),
            pltpu.VMEM((ROWS_IN, WIDTH + BLOCK), jnp.float32),
            pltpu.VMEM((NBASIS * ROWS_IN, WIDTH), jnp.bfloat16),
            pltpu.VMEM((NBASIS * ROWS_IN, WIDTH), jnp.bfloat16),
            pltpu.VMEM((ROWS_MID, WIDTH), jnp.float32),
            pltpu.SMEM((block_count,), jnp.int32),
            pltpu.SMEM((devices,), jnp.int32),
        ],
        compiler_params=pltpu.CompilerParams(dimension_semantics=("arbitrary",)),
    )(
        block_patch.reshape(-1),
        patch_owner,
        basis_taps.reshape(-1),
        psf_coef.reshape(-1),
        affine.reshape(-1),
        above,
        images,
        below,
    )
    got = pl.pallas_call(
        functools.partial(trade_kernel, devices),
        out_shape=jax.ShapeDtypeStruct((devices, capacity, BLOCK, BLOCK), jnp.bfloat16),
        in_specs=[anywhere],
        out_specs=anywhere,
        scratch_shapes=[
            pltpu.SemaphoreType.DMA((devices,)),
            pltpu.SemaphoreType.DMA((devices,)),
            pltpu.SemaphoreType.DMA,
        ],
        compiler_params=pltpu.CompilerParams(collective_id=2, has_side_effects=True),
    )(send.reshape(devices, capacity, BLOCK, BLOCK))
    size = PSIDE * BLOCK
    return pl.pallas_call(
        functools.partial(gather_kernel, devices, capacity),
        out_shape=jax.ShapeDtypeStruct((1, size, size), jnp.float32),
        in_specs=[scalars, scalars, scalars, vector],
        out_specs=vector,
        scratch_shapes=[
            pltpu.VMEM((PSIDE * PSIDE, BLOCK, BLOCK), jnp.float32),
            pltpu.SMEM((PSIDE * PSIDE,), jnp.float32),
        ],
    )(metas, patch_owner, visit_weight.astype(jnp.float32).reshape(-1), got.reshape(out_shape))


def solution(mesh):
    placed = (
        P(None, ("group", "ccd"), None),
        P(),
        P(None, "group", None, None),
        P(None, "group", None, None),
        P(None, "group"),
        P(("group", "ccd"), None, None),
        P(("group", "ccd"), None),
        P("group"),
    )
    return jax.shard_map(
        shards,
        mesh=mesh,
        in_specs=placed,
        out_specs=P(("group", "ccd"), None, None),
        check_vma=False,
    )
```

time: 76.9 us -> 65.8 us (0.86)
  the two profiles are of different devices: /device:TPU:11 before, /device:TPU:0 now
where the time goes in v1:
time: 65.8 us; the launch traced here: 64.9 us
  Pallas kernels  59.8 us (91%)
  local copies, waits for them, and re-layouts  4.37 us (7%)
  other arithmetic  0.75 us (1%)
    pallas_call x1, Pallas kernels, shards(): pl.pallas_call(functools.partial(trade_kernel, devices), out_shape=jax.Sh...  25.6 us
    pallas_call x1, Pallas kernels, shards(): pl.pallas_call(functools.partial(band_kernel, devices, capacity), out_sha...  18.3 us
    pallas_call x1, Pallas kernels, shards(): pl.pallas_call(functools.partial(rim_kernel, devices), out_shape=(rim_sha...  10.8 us
    pallas_call x1, Pallas kernels, shards(): pl.pallas_call(functools.partial(gather_kernel, devices, capacity), out_s...  5.04 us
    reshape x1, local copies, waits for them, and re-layouts, shards(): visit_weight.astype(jnp.float32).reshape(-1)  1.35 us

profile of v1, /device:TPU:0, one launch (start us, length us, event | category | flops | bytes accessed | tf_op | source)
XLA Modules:
  0.0 64.9 jit_solution(17057205603229418333)
XLA Ops:
  0.0 0.0 copy-start.1
  0.0 1.4 %reshape.29.weight_ref = f32[20]{0:T(128)} reshape(bf16[4,5]{1,0:T(4,128)(2,1)} %param.12) | data formatting | bytes 120 | tf_op jit(solution)/shard_map/reshape | solution.py:384
  1.4 0.7 %pad_add_fusion = s32[32]{0:T(128)S(1)} fusion(s32[16]{0:T(128)} %bitcast.10, s32[16]{0:T(128)} %bitcast.8), kind=kLoop, calls=%fused_computation | loop fusion | flops 32 | bytes 256 | tf_op jit(solution)/shard_map/concatenate | solution.py:312
  2.1 0.5 pad_bitcast_fusion.meta_ref
  2.6 0.0 copy-done.1
  2.6 0.0 copy-start.2
  2.6 0.6 reshape.23.taps_ref
  3.3 0.1 copy-done.2
  3.3 0.1 copy.12
  3.5 0.6 reshape.25.affine_ref
  4.1 0.0 copy-start
  4.1 10.8 %shard_map.82 = (f32[4,8,512]{2,1,0:T(8,128)}, f32[4,8,512]{2,1,0:T(8,128)}, s32[16,1,128]{2,1,0:T(1,128)}) custom-call(f32[4,128,512]{2,1,0:T(8,128)} %image_ref.3, s32[1,128]{1,0:T(1,128)} %pad_bitcast_fusion.meta_ref), custom_call_target="tpu_custom_call" | custom-call | tf_op jit(solution)/shard_map/pallas_call | solution.py:315
  14.9 0.0 copy-done
  14.9 0.2 copy.11
  15.2 0.8 %reshape.24.coef_ref = f32[540]{0:T(1024)} reshape(f32[4,5,9,3]{3,2,1,0:T(8,128)S(1)} %copy.11) | data formatting | bytes 4320 | tf_op jit(solution)/shard_map/reshape | solution.py:356
  16.0 18.3 %shard_map.83 = bf16[32,128,128]{2,1,0:T(8,128)(2,1)} custom-call(s32[16]{0:T(128)} %bitcast.9, s32[16]{0:T(128)} %owner_ref.3, f32[198]{0:T(256)} %reshape.23.taps_ref, f32[540]{0:T(1024)} %reshape.24.coef_ref, f32[80]{0:T(128)} %reshape.25.affine_ref, f32[4,8,512]{2,1,0:T(8,128)} %get-tuple-element.9.above_ref, f32[4,128,512]{2,1,0:T(8,128)} %image_ref.3, ...), custom_call_target="tpu_custom_call" | custom-call | tf_op jit(solution)/shard_map/pallas_call | solution.py:333
  34.3 25.6 %shard_map.84 = bf16[16,2,128,128]{3,2,1,0:T(8,128)(2,1)} custom-call(bf16[16,2,128,128]{3,2,1,0:T(8,128)(2,1)} %bitcast.6), custom_call_target="tpu_custom_call" | custom-call | tf_op jit(solution)/shard_map/pallas_call | solution.py:362
  59.9 5.0 %shard_map.85 = f32[1,512,512]{2,1,0:T(8,128)} custom-call(s32[16,1,128]{2,1,0:T(1,128)} %get-tuple-element.8.meta_ref, s32[16]{0:T(128)} %owner_ref.3, f32[20]{0:T(128)} %reshape.29.weight_ref, bf16[32,128,128]{2,1,0:T(8,128)(2,1)} %bitcast.7), custom_call_target="tpu_custom_call" | custom-call | tf_op jit(solution)/shard_map/pallas_call | solution.py:375
  (1 shorter events, 0.0 us)
Async XLA Ops:
  0.0 2.6 %copy-start.1 = (f32[2,9,11]{2,0,1:T(2,128)S(1)}, f32[2,9,11]{2,0,1:T(2,128)}, u32[]{:S(2)}) copy-start(f32[2,9,11]{2,0,1:T(2,128)} %param.9) | copy-start | bytes 2380
  2.6 0.7 %copy-start.2 = (f32[4,5,2,2]{1,3,2,0:T(2,128)S(1)}, f32[4,5,2,2]{1,3,2,0:T(2,128)}, u32[]{:S(2)}) copy-start(f32[4,5,2,2]{1,3,2,0:T(2,128)} %param.11) | copy-start | bytes 964
  4.1 10.8 %copy-start = (f32[4,5,9,3]{2,0,3,1:T(4,128)S(1)}, f32[4,5,9,3]{2,0,3,1:T(4,128)}, u32[]{:S(2)}) copy-start(f32[4,5,9,3]{2,0,3,1:T(4,128)} %param.10) | copy-start | bytes 6484

commit v2 on v1

--- a/solution.py
+++ b/solution.py
@@ -52,38 +52,64 @@
     pl.semaphore_wait(barrier, count - 1)
 
 
-def rim_kernel(count, image_ref, meta_ref, above_ref, below_ref, metas_ref, sent, received, rims, own):
+def rim_kernel(count, image_ref, above_ref, below_ref, rims):
     me = lax.axis_index("ccd")
-    meet(me, count)
-
-    def remote(source, target, send, receive, step):
+    barrier = pltpu.get_barrier_semaphore()
+    has_next, has_last = me < count - 1, me > 0
+
+    def to_next():
         return pltpu.make_async_remote_copy(
-            src_ref=source,
-            dst_ref=target,
-            send_sem=send,
-            recv_sem=receive,
-            device_id={"ccd": lax.rem(me + step, count)},
+            src_ref=image_ref.at[:, pl.ds(BLOCK - RIM, RIM)],
+            dst_ref=above_ref,
+            send_sem=rims.at[0],
+            recv_sem=rims.at[1],
+            device_id={"ccd": lax.rem(me + 1, count)},
             device_id_type=pl.DeviceIdType.MESH,
         )
 
-    copies = [
-        remote(image_ref.at[:, pl.ds(BLOCK - RIM, RIM)], above_ref, rims.at[0], rims.at[1], 1),
-        remote(image_ref.at[:, pl.ds(0, RIM)], below_ref, rims.at[2], rims.at[3], count - 1),
-    ]
-    for step in outward(count):
-        copies.append(
-            remote(meta_ref, metas_ref.at[me], sent.at[step], received.at[step], step)
-        )
-    for copy in copies:
-        copy.start()
-    local = pltpu.make_async_copy(meta_ref, metas_ref.at[me], own)
-    local.start()
-    local.wait()
-    for copy in copies:
-        copy.wait()
-
-
-def trade_kernel(count, send_ref, got_ref, sent, received, own):
+    def to_last():
+        return pltpu.make_async_remote_copy(
+            src_ref=image_ref.at[:, pl.ds(0, RIM)],
+            dst_ref=below_ref,
+            send_sem=rims.at[2],
+            recv_sem=rims.at[3],
+            device_id={"ccd": lax.rem(me + count - 1, count)},
+            device_id_type=pl.DeviceIdType.MESH,
+        )
+
+    for present, step in ((has_next, 1), (has_last, count - 1)):
+
+        @pl.when(present)
+        def _(step=step):
+            pl.semaphore_signal(
+                barrier,
+                inc=1,
+                device_id={"ccd": lax.rem(me + step, count)},
+                device_id_type=pl.DeviceIdType.MESH,
+            )
+
+    pl.semaphore_wait(barrier, has_next.astype(jnp.int32) + has_last.astype(jnp.int32))
+
+    @pl.when(has_next)
+    def _():
+        to_next().start()
+
+    @pl.when(has_last)
+    def _():
+        to_last().start()
+
+    @pl.when(has_next)
+    def _():
+        to_next().wait_send()
+        to_last().wait_recv()
+
+    @pl.when(has_last)
+    def _():
+        to_last().wait_send()
+        to_next().wait_recv()
+
+
+def trade_kernel(count, meta_ref, send_ref, metas_ref, got_ref, sent, received, own):
     me = lax.axis_index("ccd")
     meet(me, count)
     copies = []
@@ -93,17 +119,31 @@
             pltpu.make_async_remote_copy(
                 src_ref=send_ref.at[peer],
                 dst_ref=got_ref.at[me],
-                send_sem=sent.at[step],
-                recv_sem=received.at[step],
+                send_sem=sent.at[0, step],
+                recv_sem=received.at[0, step],
                 device_id={"ccd": peer},
                 device_id_type=pl.DeviceIdType.MESH,
             )
         )
+    for step in outward(count):
+        copies.append(
+            pltpu.make_async_remote_copy(
+                src_ref=meta_ref,
+                dst_ref=metas_ref.at[me],
+                send_sem=sent.at[1, step],
+                recv_sem=received.at[1, step],
+                device_id={"ccd": lax.rem(me + step, count)},
+                device_id_type=pl.DeviceIdType.MESH,
+            )
+        )
     for copy in copies:
         copy.start()
-    local = pltpu.make_async_copy(send_ref.at[me], got_ref.at[me], own)
-    local.start()
-    local.wait()
+    own_blocks = pltpu.make_async_copy(send_ref.at[me], got_ref.at[me], own.at[0])
+    own_meta = pltpu.make_async_copy(meta_ref, metas_ref.at[me], own.at[1])
+    own_blocks.start()
+    own_meta.start()
+    own_blocks.wait()
+    own_meta.wait()
     for copy in copies:
         copy.wait()
 
@@ -312,19 +352,14 @@
         jnp.concatenate([block_patch[0, :, 0], block_slot[0]]), (0, lanes - 2 * block_count)
     )[None]
     rim_shape = jax.ShapeDtypeStruct((V, RIM, WIDTH), jnp.float32)
-    above, below, metas = pl.pallas_call(
+    above, below = pl.pallas_call(
         functools.partial(rim_kernel, devices),
-        out_shape=(rim_shape, rim_shape, jax.ShapeDtypeStruct((devices, 1, lanes), jnp.int32)),
-        in_specs=[anywhere, vector],
-        out_specs=(anywhere, anywhere, vector),
-        scratch_shapes=[
-            pltpu.SemaphoreType.DMA((devices,)),
-            pltpu.SemaphoreType.DMA((devices,)),
-            pltpu.SemaphoreType.DMA((4,)),
-            pltpu.SemaphoreType.DMA,
-        ],
+        out_shape=(rim_shape, rim_shape),
+        in_specs=[anywhere],
+        out_specs=(anywhere, anywhere),
+        scratch_shapes=[pltpu.SemaphoreType.DMA((4,))],
         compiler_params=pltpu.CompilerParams(collective_id=1, has_side_effects=True),
-    )(images, meta)
+    )(images)
 
     def per_visit(shape):
         return pl.BlockSpec((1,) + shape[1:], lambda v: (v, 0, 0))
@@ -359,18 +394,21 @@
         images,
         below,
     )
-    got = pl.pallas_call(
+    metas, got = pl.pallas_call(
         functools.partial(trade_kernel, devices),
-        out_shape=jax.ShapeDtypeStruct((devices, capacity, BLOCK, BLOCK), jnp.bfloat16),
-        in_specs=[anywhere],
-        out_specs=anywhere,
+        out_shape=(
+            jax.ShapeDtypeStruct((devices, 1, lanes), jnp.int32),
+            jax.ShapeDtypeStruct((devices, capacity, BLOCK, BLOCK), jnp.bfloat16),
+        ),
+        in_specs=[vector, anywhere],
+        out_specs=(vector, anywhere),
         scratch_shapes=[
-            pltpu.SemaphoreType.DMA((devices,)),
-            pltpu.SemaphoreType.DMA((devices,)),
-            pltpu.SemaphoreType.DMA,
+            pltpu.SemaphoreType.DMA((2, devices)),
+            pltpu.SemaphoreType.DMA((2, devices)),
+            pltpu.SemaphoreType.DMA((2,)),
         ],
         compiler_params=pltpu.CompilerParams(collective_id=2, has_side_effects=True),
-    )(send.reshape(devices, capacity, BLOCK, BLOCK))
+    )(meta, send.reshape(devices, capacity, BLOCK, BLOCK))
     size = PSIDE * BLOCK
     return pl.pallas_call(
         functools.partial(gather_kernel, devices, capacity),

time: 65.8 us -> 66.1 us (level)
  Pallas kernels: 59.8 us -> 60.7 us
  other arithmetic: 0.75 us -> 0.07 us
    pallas_call x1, Pallas kernels: 25.6 us -> 33.1 us  [shards(): pl.pallas_call(functools.partial(trade_kernel, devices), out_shape=(jax.S...]
    pallas_call x1, Pallas kernels: 10.8 us -> 4.23 us  [shards(): pl.pallas_call(functools.partial(rim_kernel, devices), out_shape=(rim_sha...]
    unnamed x9 -> x15, local copies, waits for them, and re-layouts: 0.45 us -> 1.82 us
    reshape x1, local copies, waits for them, and re-layouts: 1.35 us -> 0.61 us  [shards(): visit_weight.astype(jnp.float32).reshape(-1)]
    concatenate x1, other arithmetic: 0.75 us -> 0.07 us  [shards(): jnp.concatenate([block_patch[0, :, 0], block_slot[0]])]
where the time goes in v2:
time: 66.1 us; the launch traced here: 65.8 us
  Pallas kernels  60.7 us (92%)
  local copies, waits for them, and re-layouts  5.03 us (8%)
    pallas_call x1, Pallas kernels, shards(): pl.pallas_call(functools.partial(trade_kernel, devices), out_shape=(jax.S...  33.1 us
    pallas_call x1, Pallas kernels, shards(): pl.pallas_call(functools.partial(band_kernel, devices, capacity), out_sha...  18.3 us
    pallas_call x1, Pallas kernels, shards(): pl.pallas_call(functools.partial(gather_kernel, devices, capacity), out_s...  5.04 us
    pallas_call x1, Pallas kernels, shards(): pl.pallas_call(functools.partial(rim_kernel, devices), out_shape=(rim_sha...  4.23 us
    unnamed x15, local copies, waits for them, and re-layouts  1.82 us

profile of v2, /device:TPU:0, one launch (start us, length us, event | category | flops | bytes accessed | tf_op | source)
XLA Modules:
  0.0 65.8 jit_solution(9042103006335958874)
XLA Ops:
  0.0 0.0 copy-start
  0.0 4.2 %shard_map.82 = (f32[4,8,512]{2,1,0:T(8,128)}, f32[4,8,512]{2,1,0:T(8,128)}) custom-call(f32[4,128,512]{2,1,0:T(8,128)} %image_ref.3), custom_call_target="tpu_custom_call" | custom-call | tf_op jit(solution)/shard_map/pallas_call | solution.py:355
  4.2 0.0 copy-done
  4.3 0.2 copy.11
  4.5 0.0 copy-start.2
  4.5 0.8 %reshape.22.coef_ref = f32[540]{0:T(1024)} reshape(f32[4,5,9,3]{3,2,1,0:T(8,128)S(1)} %copy.11) | data formatting | bytes 4320 | tf_op jit(solution)/shard_map/reshape | solution.py:391
  5.3 0.0 copy-done.2
  5.3 0.1 copy.12
  5.4 0.0 copy-start.1
  5.4 0.6 reshape.23.affine_ref
  6.0 0.1 copy-done.1
  6.1 0.7 %reshape.21.taps_ref = f32[198]{0:T(256)} reshape(f32[2,9,11]{2,1,0:T(8,128)S(1)} %copy.10) | data formatting | bytes 1584 | tf_op jit(solution)/shard_map/reshape | solution.py:390
  6.8 18.3 %shard_map.83 = bf16[32,128,128]{2,1,0:T(8,128)(2,1)} custom-call(s32[16]{0:T(128)} %bitcast.8, s32[16]{0:T(128)} %owner_ref.3, f32[198]{0:T(256)} %reshape.21.taps_ref, f32[540]{0:T(1024)} %reshape.22.coef_ref, f32[80]{0:T(128)} %reshape.23.affine_ref, f32[4,8,512]{2,1,0:T(8,128)} %get-tuple-element.9.above_ref, f32[4,128,512]{2,1,0:T(8,128)} %image_ref.3, ...), custom_call_target="tpu_custom_call" | custom-call | tf_op jit(solution)/shard_map/pallas_call | solution.py:368
  25.1 0.0 copy-start.3
  25.1 0.0 copy-start.5
  25.1 0.7 copy-done.3
  25.7 0.0 copy-done.5
  25.7 0.1 pad_add_fusion
  25.8 0.5 pad_bitcast_fusion.meta_ref
  26.4 33.1 %shard_map.84 = (s32[16,1,128]{2,1,0:T(1,128)}, bf16[16,2,128,128]{3,2,1,0:T(8,128)(2,1)}) custom-call(s32[1,128]{1,0:T(1,128)} %pad_bitcast_fusion.meta_ref, bf16[16,2,128,128]{3,2,1,0:T(8,128)(2,1)} %bitcast.6), custom_call_target="tpu_custom_call" | custom-call | tf_op jit(solution)/shard_map/pallas_call | solution.py:397
  59.5 0.0 copy-start.4
  59.5 0.7 %copy-done.4 = bf16[4,5]{1,0:T(4,128)(2,1)S(1)} copy-done((bf16[4,5]{1,0:T(4,128)(2,1)S(1)}, bf16[4,5]{1,0:T(4,128)(2,1)}, u32[]{:S(2)}) %copy-start.4) | copy-done | bytes 64
  60.2 0.6 reshape.29.weight_ref
  60.8 5.0 %shard_map.85 = f32[1,512,512]{2,1,0:T(8,128)} custom-call(s32[16,1,128]{2,1,0:T(1,128)} %get-tuple-element.11.meta_ref, s32[16]{0:T(128)} %owner_ref.3, f32[20]{0:T(128)} %reshape.29.weight_ref, bf16[32,128,128]{2,1,0:T(8,128)(2,1)} %bitcast.7), custom_call_target="tpu_custom_call" | custom-call | tf_op jit(solution)/shard_map/pallas_call | solution.py:413
  (1 shorter events, 0.0 us)
Async XLA Ops:
  0.0 4.2 %copy-start = (f32[4,5,9,3]{2,0,3,1:T(4,128)S(1)}, f32[4,5,9,3]{2,0,3,1:T(4,128)}, u32[]{:S(2)}) copy-start(f32[4,5,9,3]{2,0,3,1:T(4,128)} %param.10) | copy-start | bytes 6484
  4.5 0.8 %copy-start.2 = (f32[4,5,2,2]{1,3,2,0:T(2,128)S(1)}, f32[4,5,2,2]{1,3,2,0:T(2,128)}, u32[]{:S(2)}) copy-start(f32[4,5,2,2]{1,3,2,0:T(2,128)} %param.11) | copy-start | bytes 964
  5.4 0.7 %copy-start.1 = (f32[2,9,11]{2,0,1:T(2,128)S(1)}, f32[2,9,11]{2,0,1:T(2,128)}, u32[]{:S(2)}) copy-start(f32[2,9,11]{2,0,1:T(2,128)} %param.9) | copy-start | bytes 2380
  25.1 0.7 copy-start.3
  25.1 0.7 %copy-start.5 = (s32[1,16]{1,0:T(1,128)S(1)}, s32[1,16]{1,0:T(1,128)}, u32[]{:S(2)}) copy-start(s32[1,16]{1,0:T(1,128)} %param.14) | copy-start | bytes 196
  59.5 0.7 %copy-start.4 = (bf16[4,5]{1,0:T(4,128)(2,1)S(1)}, bf16[4,5]{1,0:T(4,128)(2,1)}, u32[]{:S(2)}) copy-start(bf16[4,5]{1,0:T(4,128)(2,1)} %param.12) | copy-start | bytes 124

commit v3 on v2

v3 whole, which is shorter than its diff:
```python
import functools

import jax
import jax.numpy as jnp
from jax import lax
from jax.experimental import pallas as pl
from jax.experimental.pallas import tpu as pltpu
from jax.sharding import PartitionSpec as P

V = 4
BLOCK = 128
BLKC = 4
SPLIT = 4
TAPS = 11
NBASIS = 9
PSIDE = 4
HALF = TAPS // 2
REACH = 3
RIM = HALF + REACH
CHUNKS = 2
CHUNK = BLOCK // CHUNKS
ROWS_IN = CHUNK + 2 * RIM
ROWS_MID = CHUNK + 8
WIDTH = BLKC * BLOCK
HEIGHT = SPLIT * BLOCK
LEFT = BLOCK // 2
STEPS = 2 * REACH + 1


def sinc(values):
    angle = jnp.pi * values
    zero = values == 0.0
    return jnp.where(zero, 1.0, jnp.sin(angle) / jnp.where(zero, 1.0, angle))


def lanczos(offset):
    inside = jnp.abs(offset) < 3.0
    return jnp.where(inside, sinc(offset) * sinc(offset / 3.0), 0.0)


def outward(count):
    return sorted(range(1, count), key=lambda step: abs(step - count // 2))


def rim_kernel(count, image_ref, above_ref, below_ref, rims):
    me = lax.axis_index("ccd")
    barrier = pltpu.get_barrier_semaphore()
    has_next, has_last = me < count - 1, me > 0

    def to_next():
        return pltpu.make_async_remote_copy(
            src_ref=image_ref.at[:, pl.ds(BLOCK - RIM, RIM)],
            dst_ref=above_ref,
            send_sem=rims.at[0],
            recv_sem=rims.at[1],
            device_id={"ccd": lax.rem(me + 1, count)},
            device_id_type=pl.DeviceIdType.MESH,
        )

    def to_last():
        return pltpu.make_async_remote_copy(
            src_ref=image_ref.at[:, pl.ds(0, RIM)],
            dst_ref=below_ref,
            send_sem=rims.at[2],
            recv_sem=rims.at[3],
            device_id={"ccd": lax.rem(me + count - 1, count)},
            device_id_type=pl.DeviceIdType.MESH,
        )

    for present, step in ((has_next, 1), (has_last, count - 1)):

        @pl.when(present)
        def _(step=step):
            pl.semaphore_signal(
                barrier,
                inc=1,
                device_id={"ccd": lax.rem(me + step, count)},
                device_id_type=pl.DeviceIdType.MESH,
            )

    pl.semaphore_wait(barrier, has_next.astype(jnp.int32) + has_last.astype(jnp.int32))

    @pl.when(has_next)
    def _():
        to_next().start()

    @pl.when(has_last)
    def _():
        to_last().start()

    @pl.when(has_next)
    def _():
        to_next().wait_send()
        to_last().wait_recv()

    @pl.when(has_last)
    def _():
        to_last().wait_send()
        to_next().wait_recv()


def split(values):
    high = values.astype(jnp.bfloat16)
    return high, (values - high.astype(jnp.float32)).astype(jnp.bfloat16)


def dot(left, right):
    return jnp.dot(left, right, preferred_element_type=jnp.float32)


def plan_kernel(devices, capacity, patch_ref, owner_ref, block_ref, filled):
    for device in range(devices):
        filled[device] = 0
    for slot in range(devices * capacity):
        block_ref[slot] = 0
    for block in range(V * BLKC):
        device = owner_ref[patch_ref[block]]
        block_ref[device * capacity + filled[device]] = block
        filled[device] = filled[device] + 1


def band_kernel(
    devices,
    capacity,
    block_ref,
    taps_ref,
    coef_ref,
    affine_ref,
    meta_ref,
    above_ref,
    image_ref,
    below_ref,
    metas_ref,
    got_ref,
    col_high,
    col_low,
    row_kernel,
    wide,
    terms_high,
    terms_low,
    mid,
    stage,
    outbox,
    sent,
    received,
    own,
):
    band = lax.axis_index("ccd")
    barrier = pltpu.get_barrier_semaphore()
    for step in range(1, devices):
        pl.semaphore_signal(
            barrier,
            inc=1,
            device_id={"ccd": lax.rem(band + step, devices)},
            device_id_type=pl.DeviceIdType.MESH,
        )
    shifted = band + SPLIT // 2
    ccd = shifted // SPLIT
    top_row = shifted % SPLIT * BLOCK
    region_shift = band * BLOCK - top_row
    region_low = jnp.maximum(0, -region_shift)
    region_high = jnp.minimum(HEIGHT, devices * BLOCK - region_shift)
    ccds = coef_ref.shape[0] // (V * NBASIS * 3)
    wide_lane = lax.broadcasted_iota(jnp.int32, (1, NBASIS * ROWS_IN), 1)

    def by_basis(value):
        total = jnp.full((1, NBASIS * ROWS_IN), value(0), jnp.float32)
        for basis in range(1, NBASIS):
            total = jnp.where(wide_lane >= basis * ROWS_IN, value(basis), total)
        return total

    def inside(first, count):
        rows = first + lax.broadcasted_iota(jnp.int32, (count, 1), 0)
        return (rows >= region_low) & (rows < region_high)

    depth = lax.broadcasted_iota(jnp.int32, (2 * BLOCK, BLOCK), 0)
    lane = lax.broadcasted_iota(jnp.int32, (2 * BLOCK, BLOCK), 1)
    distance = depth - (LEFT - HALF) - lane
    for basis in range(NBASIS):
        cols = pl.ds(basis * BLOCK, BLOCK)
        total = jnp.zeros((2 * BLOCK, BLOCK), jnp.float32)
        for tap in range(TAPS):
            total = jnp.where(
                distance == tap, taps_ref[(NBASIS + basis) * TAPS + tap], total
            )
        high, low = split(total)
        col_high[:, cols] = high
        col_low[:, cols] = low
    start = jnp.zeros((1, NBASIS * ROWS_IN), jnp.int32)
    for basis in range(1, NBASIS):
        start = jnp.where(wide_lane >= basis * ROWS_IN, basis * ROWS_IN, start)
    gap = (wide_lane - start) - lax.broadcasted_iota(
        jnp.int32, (ROWS_MID, NBASIS * ROWS_IN), 0
    )
    total = jnp.zeros(gap.shape, jnp.float32)
    for tap in range(TAPS):
        total = jnp.where(
            gap == tap, by_basis(lambda basis: taps_ref[basis * TAPS + tap]), total
        )
    row_kernel[...] = total
    wide[...] = jnp.zeros_like(wide)

    column = lax.broadcasted_iota(jnp.int32, (1, WIDTH), 1).astype(jnp.float32)
    col_pos = (2.0 * column + 1.0) / WIDTH - 1.0

    def remote(source, target, kind, step):
        return pltpu.make_async_remote_copy(
            src_ref=source,
            dst_ref=target,
            send_sem=sent.at[kind, step],
            recv_sem=received.at[kind, step],
            device_id={"ccd": lax.rem(band + step, devices)},
            device_id_type=pl.DeviceIdType.MESH,
        )

    pl.semaphore_wait(barrier, devices - 1)
    copies = [
        remote(meta_ref, metas_ref.at[band], CHUNKS, step) for step in outward(devices)
    ]
    locals_ = [pltpu.make_async_copy(meta_ref, metas_ref.at[band], own.at[CHUNKS])]
    for copy in copies + locals_:
        copy.start()
    for chunk in range(CHUNKS):
        first = top_row + chunk * CHUNK

        def one_visit(visit, carry, chunk=chunk, first=first):
            place = visit * ccds + ccd
            raw = jnp.concatenate([above_ref[visit], image_ref[visit], below_ref[visit]], axis=0)
            raw = raw[chunk * CHUNK : chunk * CHUNK + ROWS_IN]
            raw = jnp.where(inside(first - RIM, ROWS_IN), raw, 0.0)
            wide[:, LEFT : LEFT + WIDTH] = raw
            for block in range(BLKC):
                high, low = split(wide[:, block * BLOCK : (block + 2) * BLOCK])
                term = dot(high, col_high[...]) + dot(low, col_high[...]) + dot(high, col_low[...])
                high, low = split(term)
                for basis in range(NBASIS):
                    rows = pl.ds(basis * ROWS_IN, ROWS_IN)
                    cols = pl.ds(block * BLOCK, BLOCK)
                    terms_high[rows, cols] = high[:, basis * BLOCK : (basis + 1) * BLOCK]
                    terms_low[rows, cols] = low[:, basis * BLOCK : (basis + 1) * BLOCK]

            position = (first - REACH + lax.broadcasted_iota(jnp.int32, (ROWS_MID, 1), 0)).astype(
                jnp.float32
            )
            row_pos = (2.0 * position + 1.0) / HEIGHT - 1.0
            kernel = row_kernel[...]
            constant, by_row, by_column = (
                by_basis(lambda basis: coef_ref[(place * NBASIS + basis) * 3 + part]) for part in range(3)
            )
            level = kernel * (constant + by_row * row_pos)
            slope = kernel * by_column
            level_high, level_low = split(level)
            slope_high, slope_low = split(slope)
            upper = dot(
                jnp.concatenate([level_high, slope_high, level_low, slope_low], axis=0), terms_high[...]
            )
            lower = dot(jnp.concatenate([level_high, slope_high], axis=0), terms_low[...])
            both = upper[: 2 * ROWS_MID] + upper[2 * ROWS_MID :] + lower
            matched = both[:ROWS_MID] + both[ROWS_MID:] * col_pos
            mid[...] = jnp.where(inside(first - REACH, ROWS_MID), matched, 0.0)

            own_rows = (first + lax.broadcasted_iota(jnp.int32, (CHUNK, 1), 0)).astype(jnp.float32)
            row_shift = affine_ref[place * 4] + affine_ref[place * 4 + 1] * (
                (own_rows - (HEIGHT - 1) / 2.0) / HEIGHT
            )
            row_step = lax.broadcasted_iota(jnp.int32, (CHUNK, BLOCK), 1) - REACH
            row_weight = lanczos(row_shift - row_step.astype(jnp.float32))
            col_shift = affine_ref[place * 4 + 2] + affine_ref[place * 4 + 3] * (
                (column - (WIDTH - 1) / 2.0) / WIDTH
            )
            col_step = lax.broadcasted_iota(jnp.int32, (8, WIDTH), 0) - REACH
            reached = lax.broadcasted_iota(jnp.int32, (8, WIDTH), 1) + col_step
            col_weight = jnp.where(
                (reached >= 0) & (reached < WIDTH),
                lanczos(col_shift - col_step.astype(jnp.float32)),
                0.0,
            )
            warped = jnp.zeros((CHUNK, WIDTH), jnp.float32)
            for step in range(STEPS):
                warped = warped + row_weight[:, step : step + 1] * mid[step : step + CHUNK, :]
            total = jnp.zeros((CHUNK, WIDTH), jnp.float32)
            for step in range(STEPS):
                offset = step - REACH
                moved = warped if offset == 0 else pltpu.roll(warped, (-offset) % WIDTH, 1)
                total = total + col_weight[step : step + 1, :] * moved
            rounded = total.astype(jnp.bfloat16)
            for block in range(BLKC):
                stage[chunk * V * BLKC + visit * BLKC + block] = rounded[
                    :, block * BLOCK : (block + 1) * BLOCK
                ]
            return carry

        lax.fori_loop(0, V, one_visit, 0)
        for device in range(devices):
            for slot in range(capacity):
                outbox[chunk, device, slot] = stage[
                    chunk * V * BLKC + block_ref[device * capacity + slot]
                ]
        batch = [
            remote(
                outbox.at[chunk, lax.rem(band + step, devices)],
                got_ref.at[chunk, band],
                chunk,
                step,
            )
            for step in outward(devices)
        ]
        local = pltpu.make_async_copy(
            outbox.at[chunk, band], got_ref.at[chunk, band], own.at[chunk]
        )
        for copy in batch + [local]:
            copy.start()
        copies += batch
        locals_.append(local)
    for copy in locals_ + copies:
        copy.wait()


def gather_kernel(devices, capacity, meta_ref, owner_ref, weight_ref, got_ref, out_ref, total, weights):
    me = lax.axis_index("ccd")
    total[...] = jnp.zeros_like(total)
    for cell in range(PSIDE * PSIDE):
        weights[cell] = 0.0
    patch = jnp.int32(0)
    for candidate in range(owner_ref.shape[0]):
        patch = jnp.where(owner_ref[candidate] == me, candidate, patch)
    ccds = weight_ref.shape[0] // V
    count = V * BLKC

    def add(source, carry):
        ccd = (source + SPLIT // 2) // SPLIT
        taken = source * capacity
        for block in range(count):
            mine = meta_ref[source, 0, block] == patch

            @pl.when(mine)
            def _(taken=taken, block=block):
                cell = meta_ref[source, 0, count + block]
                weight = weight_ref[block // BLKC * ccds + ccd]
                weights[cell] = weights[cell] + weight
                for chunk in range(CHUNKS):
                    rows = pl.ds(chunk * CHUNK, CHUNK)
                    total[cell, rows] = total[cell, rows] + weight * got_ref[
                        chunk, taken
                    ].astype(jnp.float32)

            taken = taken + mine.astype(jnp.int32)
        return carry

    lax.fori_loop(0, devices, add, 0)
    for cell in range(PSIDE * PSIDE):
        row, col = cell // PSIDE * BLOCK, cell % PSIDE * BLOCK
        scale = jnp.full((1, BLOCK), jnp.maximum(weights[cell], 1.0), jnp.float32)
        out_ref[0, row : row + BLOCK, col : col + BLOCK] = total[cell] / scale


def shards(
    images, basis_taps, psf_coef, affine, visit_weight, block_patch, block_slot, patch_owner
):
    devices = lax.axis_size("ccd")
    block_count = V * BLKC
    capacity = max(2, (2 * block_count + devices - 1) // devices)
    slots = devices * capacity
    anywhere = pl.BlockSpec(memory_space=pl.ANY)
    scalars = pl.BlockSpec(memory_space=pltpu.SMEM)
    vector = pl.BlockSpec(memory_space=pltpu.VMEM)
    lanes = -(-2 * block_count // BLOCK) * BLOCK
    meta = jnp.pad(
        jnp.concatenate([block_patch[0, :, 0], block_slot[0]]), (0, lanes - 2 * block_count)
    )[None]
    rim_shape = jax.ShapeDtypeStruct((V, RIM, WIDTH), jnp.float32)
    above, below = pl.pallas_call(
        functools.partial(rim_kernel, devices),
        out_shape=(rim_shape, rim_shape),
        in_specs=[anywhere],
        out_specs=(anywhere, anywhere),
        scratch_shapes=[pltpu.SemaphoreType.DMA((4,))],
        compiler_params=pltpu.CompilerParams(collective_id=1, has_side_effects=True),
    )(images)

    blocks = pl.pallas_call(
        functools.partial(plan_kernel, devices, capacity),
        out_shape=jax.ShapeDtypeStruct((slots,), jnp.int32),
        in_specs=[scalars, scalars],
        out_specs=scalars,
        scratch_shapes=[pltpu.SMEM((devices,), jnp.int32)],
    )(block_patch.reshape(-1), patch_owner)
    metas, got = pl.pallas_call(
        functools.partial(band_kernel, devices, capacity),
        out_shape=(
            jax.ShapeDtypeStruct((devices, 1, lanes), jnp.int32),
            jax.ShapeDtypeStruct((CHUNKS, devices, capacity, CHUNK, BLOCK), jnp.bfloat16),
        ),
        in_specs=[scalars] * 4 + [vector] * 4,
        out_specs=(vector, anywhere),
        scratch_shapes=[
            pltpu.VMEM((2 * BLOCK, NBASIS * BLOCK), jnp.bfloat16),
            pltpu.VMEM((2 * BLOCK, NBASIS * BLOCK), jnp.bfloat16),
            pltpu.VMEM((ROWS_MID, NBASIS * ROWS_IN), jnp.float32),
            pltpu.VMEM((ROWS_IN, WIDTH + BLOCK), jnp.float32),
            pltpu.VMEM((NBASIS * ROWS_IN, WIDTH), jnp.bfloat16),
            pltpu.VMEM((NBASIS * ROWS_IN, WIDTH), jnp.bfloat16),
            pltpu.VMEM((ROWS_MID, WIDTH), jnp.float32),
            pltpu.VMEM((CHUNKS * block_count, CHUNK, BLOCK), jnp.bfloat16),
            pltpu.VMEM((CHUNKS, devices, capacity, CHUNK, BLOCK), jnp.bfloat16),
            pltpu.SemaphoreType.DMA((CHUNKS + 1, devices)),
            pltpu.SemaphoreType.DMA((CHUNKS + 1, devices)),
            pltpu.SemaphoreType.DMA((CHUNKS + 1,)),
        ],
        compiler_params=pltpu.CompilerParams(collective_id=2, has_side_effects=True),
    )(
        blocks,
        basis_taps.reshape(-1),
        psf_coef.reshape(-1),
        affine.reshape(-1),
        meta,
        above,
        images,
        below,
    )
    size = PSIDE * BLOCK
    return pl.pallas_call(
        functools.partial(gather_kernel, devices, capacity),
        out_shape=jax.ShapeDtypeStruct((1, size, size), jnp.float32),
        in_specs=[scalars, scalars, scalars, vector],
        out_specs=vector,
        scratch_shapes=[
            pltpu.VMEM((PSIDE * PSIDE, BLOCK, BLOCK), jnp.float32),
            pltpu.SMEM((PSIDE * PSIDE,), jnp.float32),
        ],
    )(metas, patch_owner, visit_weight.astype(jnp.float32).reshape(-1), got.reshape(CHUNKS, slots, CHUNK, BLOCK))


def solution(mesh):
    placed = (
        P(None, ("group", "ccd"), None),
        P(),
        P(None, "group", None, None),
        P(None, "group", None, None),
        P(None, "group"),
        P(("group", "ccd"), None, None),
        P(("group", "ccd"), None),
        P("group"),
    )
    return jax.shard_map(
        shards,
        mesh=mesh,
        in_specs=placed,
        out_specs=P(("group", "ccd"), None, None),
        check_vma=False,
    )
```

time: 66.1 us -> 56.8 us (0.86)
  Pallas kernels: 60.7 us -> 51.3 us
  other arithmetic: 0.07 us -> 0.75 us
    pallas_call x1, Pallas kernels: 33.1 us -> 1.3 us  [shards(): pl.pallas_call(functools.partial(plan_kernel, devices, capacity), out_sha...]
    pallas_call x1, Pallas kernels: 18.3 us -> 40.7 us  [shards(): pl.pallas_call(functools.partial(band_kernel, devices, capacity), out_sha...]
    unnamed x15 -> x9, local copies, waits for them, and re-layouts: 1.82 us -> 0.39 us
    reshape x1, local copies, waits for them, and re-layouts: 0.61 us -> 1.37 us  [shards(): visit_weight.astype(jnp.float32).reshape(-1)]
    concatenate x1, other arithmetic: 0.07 us -> 0.75 us  [shards(): jnp.concatenate([block_patch[0, :, 0], block_slot[0]])]
where the time goes in v3:
time: 56.8 us; the launch traced here: 56.6 us
  Pallas kernels  51.3 us (90%)
  local copies, waits for them, and re-layouts  4.46 us (8%)
  other arithmetic  0.75 us (1%)
    pallas_call x1, Pallas kernels, shards(): pl.pallas_call(functools.partial(band_kernel, devices, capacity), out_sha...  40.7 us
    pallas_call x1, Pallas kernels, shards(): pl.pallas_call(functools.partial(gather_kernel, devices, capacity), out_s...  5.04 us
    pallas_call x1, Pallas kernels, shards(): pl.pallas_call(functools.partial(rim_kernel, devices), out_shape=(rim_sha...  4.23 us
    reshape x1, local copies, waits for them, and re-layouts, shards(): visit_weight.astype(jnp.float32).reshape(-1)  1.37 us
    pallas_call x1, Pallas kernels, shards(): pl.pallas_call(functools.partial(plan_kernel, devices, capacity), out_sha...  1.3 us

profile of v3, /device:TPU:0, one launch (start us, length us, event | category | flops | bytes accessed | tf_op | source)
XLA Modules:
  0.0 56.6 jit_solution(526996828988388534)
XLA Ops:
  0.0 0.0 copy-start.1
  0.0 1.4 %reshape.28.weight_ref = f32[20]{0:T(128)} reshape(bf16[4,5]{1,0:T(4,128)(2,1)} %param.12) | data formatting | bytes 120 | tf_op jit(solution)/shard_map/reshape | solution.py:431
  1.4 0.7 %pad_add_fusion = s32[32]{0:T(128)S(1)} fusion(s32[16]{0:T(128)} %bitcast.6, s32[16]{0:T(128)} %bitcast.7), kind=kLoop, calls=%fused_computation | loop fusion | flops 32 | bytes 256 | tf_op jit(solution)/shard_map/concatenate | solution.py:369
  2.1 0.6 %pad_bitcast_fusion.meta_ref = s32[1,128]{1,0:T(1,128)} fusion(s32[32]{0:T(128)S(1)} %pad_add_fusion), kind=kLoop, calls=%fused_computation.1 | loop fusion | bytes 640 | tf_op jit(solution)/shard_map/broadcast_in_dim | solution.py:368
  2.7 1.3 %shard_map.82.block_ref = s32[32]{0:T(128)} custom-call(s32[16]{0:T(128)} %bitcast.8, s32[16]{0:T(128)} %owner_ref.3), custom_call_target="tpu_custom_call" | custom-call | tf_op jit(solution)/shard_map/pallas_call | solution.py:381
  4.0 0.0 copy-done.1
  4.0 0.0 copy-start.2
  4.0 0.7 %reshape.21.taps_ref = f32[198]{0:T(256)} reshape(f32[2,9,11]{2,1,0:T(8,128)S(1)} %copy.10) | data formatting | bytes 1584 | tf_op jit(solution)/shard_map/reshape | solution.py:413
  4.7 0.0 copy-done.2
  4.7 0.1 copy.12
  4.9 0.6 %reshape.23.affine_ref = f32[80]{0:T(128)} reshape(f32[4,5,2,2]{3,2,1,0:T(2,128)S(1)} %copy.12) | data formatting | bytes 640 | tf_op jit(solution)/shard_map/reshape | solution.py:415
  5.5 0.0 copy-start
  5.5 4.2 %shard_map.83 = (f32[4,8,512]{2,1,0:T(8,128)}, f32[4,8,512]{2,1,0:T(8,128)}) custom-call(f32[4,128,512]{2,1,0:T(8,128)} %image_ref.3), custom_call_target="tpu_custom_call" | custom-call | tf_op jit(solution)/shard_map/pallas_call | solution.py:372
  9.7 0.0 copy-done
  9.8 0.2 copy.11
  10.0 0.8 %reshape.22.coef_ref = f32[540]{0:T(1024)} reshape(f32[4,5,9,3]{3,2,1,0:T(8,128)S(1)} %copy.11) | data formatting | bytes 4320 | tf_op jit(solution)/shard_map/reshape | solution.py:414
  10.8 40.7 %shard_map.84 = (s32[16,1,128]{2,1,0:T(1,128)}, bf16[2,16,2,64,128]{4,3,2,1,0:T(8,128)(2,1)}) custom-call(s32[32]{0:T(128)} %shard_map.82.block_ref, f32[198]{0:T(256)} %reshape.21.taps_ref, f32[540]{0:T(1024)} %reshape.22.coef_ref, f32[80]{0:T(128)} %reshape.23.affine_ref, s32[1,128]{1,0:T(1,128)} %pad_bitcast_fusion.meta_ref, ...), custom_call_target="tpu_custom_call" | custom-call | tf_op jit(solution)/shard_map/pallas_call | solution.py:388
  51.5 5.0 %shard_map.85 = f32[1,512,512]{2,1,0:T(8,128)} custom-call(s32[16,1,128]{2,1,0:T(1,128)} %get-tuple-element.11.meta_ref, s32[16]{0:T(128)} %owner_ref.3, f32[20]{0:T(128)} %reshape.28.weight_ref, bf16[2,32,64,128]{3,2,1,0:T(8,128)(2,1)} %bitcast.5), custom_call_target="tpu_custom_call" | custom-call | tf_op jit(solution)/shard_map/pallas_call | solution.py:422
  (1 shorter events, 0.0 us)
Async XLA Ops:
  0.0 4.0 %copy-start.1 = (f32[2,9,11]{2,0,1:T(2,128)S(1)}, f32[2,9,11]{2,0,1:T(2,128)}, u32[]{:S(2)}) copy-start(f32[2,9,11]{2,0,1:T(2,128)} %param.9) | copy-start | bytes 2380
  4.0 0.7 %copy-start.2 = (f32[4,5,2,2]{1,3,2,0:T(2,128)S(1)}, f32[4,5,2,2]{1,3,2,0:T(2,128)}, u32[]{:S(2)}) copy-start(f32[4,5,2,2]{1,3,2,0:T(2,128)} %param.11) | copy-start | bytes 964
  5.5 4.2 %copy-start = (f32[4,5,9,3]{2,0,3,1:T(4,128)S(1)}, f32[4,5,9,3]{2,0,3,1:T(4,128)}, u32[]{:S(2)}) copy-start(f32[4,5,9,3]{2,0,3,1:T(4,128)} %param.10) | copy-start | bytes 6484

commit v4 on v3

--- a/solution.py
+++ b/solution.py
@@ -17,7 +17,7 @@
 HALF = TAPS // 2
 REACH = 3
 RIM = HALF + REACH
-CHUNKS = 2
+CHUNKS = 4
 CHUNK = BLOCK // CHUNKS
 ROWS_IN = CHUNK + 2 * RIM
 ROWS_MID = CHUNK + 8

time: 56.8 us -> 60.3 us (1.062)
  Pallas kernels: 51.3 us -> 54.7 us
    pallas_call x1, Pallas kernels: 40.7 us -> 44.1 us  [shards(): pl.pallas_call(functools.partial(band_kernel, devices, capacity), out_sha...]
where the time goes in v4:
time: 60.3 us; the launch traced here: 60 us
  Pallas kernels  54.7 us (91%)
  local copies, waits for them, and re-layouts  4.46 us (7%)
  other arithmetic  0.75 us (1%)
    pallas_call x1, Pallas kernels, shards(): pl.pallas_call(functools.partial(band_kernel, devices, capacity), out_sha...  44.1 us
    pallas_call x1, Pallas kernels, shards(): pl.pallas_call(functools.partial(gather_kernel, devices, capacity), out_s...  5.06 us
    pallas_call x1, Pallas kernels, shards(): pl.pallas_call(functools.partial(rim_kernel, devices), out_shape=(rim_sha...  4.23 us
    reshape x1, local copies, waits for them, and re-layouts, shards(): visit_weight.astype(jnp.float32).reshape(-1)  1.37 us
    pallas_call x1, Pallas kernels, shards(): pl.pallas_call(functools.partial(plan_kernel, devices, capacity), out_sha...  1.3 us

profile of v4, /device:TPU:0, one launch (start us, length us, event | category | flops | bytes accessed | tf_op | source)
XLA Modules:
  0.0 60.0 jit_solution(9575434118116352305)
XLA Ops:
  0.0 0.0 copy-start.1
  0.0 1.4 %reshape.28.weight_ref = f32[20]{0:T(128)} reshape(bf16[4,5]{1,0:T(4,128)(2,1)} %param.12) | data formatting | bytes 120 | tf_op jit(solution)/shard_map/reshape | solution.py:431
  1.4 0.7 %pad_add_fusion = s32[32]{0:T(128)S(1)} fusion(s32[16]{0:T(128)} %bitcast.6, s32[16]{0:T(128)} %bitcast.7), kind=kLoop, calls=%fused_computation | loop fusion | flops 32 | bytes 256 | tf_op jit(solution)/shard_map/concatenate | solution.py:369
  2.1 0.6 pad_bitcast_fusion.meta_ref
  2.7 1.3 %shard_map.82.block_ref = s32[32]{0:T(128)} custom-call(s32[16]{0:T(128)} %bitcast.8, s32[16]{0:T(128)} %owner_ref.3), custom_call_target="tpu_custom_call" | custom-call | tf_op jit(solution)/shard_map/pallas_call | solution.py:381
  4.0 0.0 copy-done.1
  4.0 0.0 copy-start.2
  4.0 0.7 %reshape.21.taps_ref = f32[198]{0:T(256)} reshape(f32[2,9,11]{2,1,0:T(8,128)S(1)} %copy.10) | data formatting | bytes 1584 | tf_op jit(solution)/shard_map/reshape | solution.py:413
  4.7 0.0 copy-done.2
  4.7 0.1 copy.12
  4.9 0.6 %reshape.23.affine_ref = f32[80]{0:T(128)} reshape(f32[4,5,2,2]{3,2,1,0:T(2,128)S(1)} %copy.12) | data formatting | bytes 640 | tf_op jit(solution)/shard_map/reshape | solution.py:415
  5.5 0.0 copy-start
  5.5 4.2 %shard_map.83 = (f32[4,8,512]{2,1,0:T(8,128)}, f32[4,8,512]{2,1,0:T(8,128)}) custom-call(f32[4,128,512]{2,1,0:T(8,128)} %image_ref.3), custom_call_target="tpu_custom_call" | custom-call | tf_op jit(solution)/shard_map/pallas_call | solution.py:372
  9.7 0.0 copy-done
  9.8 0.2 copy.11
  10.0 0.8 %reshape.22.coef_ref = f32[540]{0:T(1024)} reshape(f32[4,5,9,3]{3,2,1,0:T(8,128)S(1)} %copy.11) | data formatting | bytes 4320 | tf_op jit(solution)/shard_map/reshape | solution.py:414
  10.8 44.1 %shard_map.84 = (s32[16,1,128]{2,1,0:T(1,128)}, bf16[4,16,2,32,128]{4,3,2,1,0:T(8,128)(2,1)}) custom-call(s32[32]{0:T(128)} %shard_map.82.block_ref, f32[198]{0:T(256)} %reshape.21.taps_ref, f32[540]{0:T(1024)} %reshape.22.coef_ref, f32[80]{0:T(128)} %reshape.23.affine_ref, s32[1,128]{1,0:T(1,128)} %pad_bitcast_fusion.meta_ref, ...), custom_call_target="tpu_custom_call" | custom-call | tf_op jit(solution)/shard_map/pallas_call | solution.py:388
  54.9 5.1 %shard_map.85 = f32[1,512,512]{2,1,0:T(8,128)} custom-call(s32[16,1,128]{2,1,0:T(1,128)} %get-tuple-element.11.meta_ref, s32[16]{0:T(128)} %owner_ref.3, f32[20]{0:T(128)} %reshape.28.weight_ref, bf16[4,32,32,128]{3,2,1,0:T(8,128)(2,1)} %bitcast.5), custom_call_target="tpu_custom_call" | custom-call | tf_op jit(solution)/shard_map/pallas_call | solution.py:422
  (1 shorter events, 0.0 us)
Async XLA Ops:
  0.0 4.0 %copy-start.1 = (f32[2,9,11]{2,0,1:T(2,128)S(1)}, f32[2,9,11]{2,0,1:T(2,128)}, u32[]{:S(2)}) copy-start(f32[2,9,11]{2,0,1:T(2,128)} %param.9) | copy-start | bytes 2380
  4.0 0.7 %copy-start.2 = (f32[4,5,2,2]{1,3,2,0:T(2,128)S(1)}, f32[4,5,2,2]{1,3,2,0:T(2,128)}, u32[]{:S(2)}) copy-start(f32[4,5,2,2]{1,3,2,0:T(2,128)} %param.11) | copy-start | bytes 964
  5.5 4.2 %copy-start = (f32[4,5,9,3]{2,0,3,1:T(4,128)S(1)}, f32[4,5,9,3]{2,0,3,1:T(4,128)}, u32[]{:S(2)}) copy-start(f32[4,5,9,3]{2,0,3,1:T(4,128)} %param.10) | copy-start | bytes 6484

commit v5 on v3

--- a/solution.py
+++ b/solution.py
@@ -108,15 +108,21 @@
     return jnp.dot(left, right, preferred_element_type=jnp.float32)
 
 
-def plan_kernel(devices, capacity, patch_ref, owner_ref, block_ref, filled):
+def plan_kernel(devices, capacity, patch_ref, slot_ref, owner_ref, block_ref, meta_ref, filled):
     for device in range(devices):
         filled[device] = 0
     for slot in range(devices * capacity):
         block_ref[slot] = 0
+    lane = lax.broadcasted_iota(jnp.int32, meta_ref.shape, 1)
+    meta = jnp.zeros(meta_ref.shape, jnp.int32)
     for block in range(V * BLKC):
-        device = owner_ref[patch_ref[block]]
+        patch = patch_ref[block]
+        meta = jnp.where(lane == block, patch, meta)
+        meta = jnp.where(lane == V * BLKC + block, slot_ref[0, block], meta)
+        device = owner_ref[patch]
         block_ref[device * capacity + filled[device]] = block
         filled[device] = filled[device] + 1
+    meta_ref[...] = meta
 
 
 def band_kernel(
@@ -181,7 +187,7 @@
         total = jnp.zeros((2 * BLOCK, BLOCK), jnp.float32)
         for tap in range(TAPS):
             total = jnp.where(
-                distance == tap, taps_ref[(NBASIS + basis) * TAPS + tap], total
+                distance == tap, taps_ref[1, basis, tap], total
             )
         high, low = split(total)
         col_high[:, cols] = high
@@ -195,7 +201,7 @@
     total = jnp.zeros(gap.shape, jnp.float32)
     for tap in range(TAPS):
         total = jnp.where(
-            gap == tap, by_basis(lambda basis: taps_ref[basis * TAPS + tap]), total
+            gap == tap, by_basis(lambda basis: taps_ref[0, basis, tap]), total
         )
     row_kernel[...] = total
     wide[...] = jnp.zeros_like(wide)
@@ -260,12 +266,12 @@
             mid[...] = jnp.where(inside(first - REACH, ROWS_MID), matched, 0.0)
 
             own_rows = (first + lax.broadcasted_iota(jnp.int32, (CHUNK, 1), 0)).astype(jnp.float32)
-            row_shift = affine_ref[place * 4] + affine_ref[place * 4 + 1] * (
+            row_shift = affine_ref[visit, ccd, 0, 0] + affine_ref[visit, ccd, 0, 1] * (
                 (own_rows - (HEIGHT - 1) / 2.0) / HEIGHT
             )
             row_step = lax.broadcasted_iota(jnp.int32, (CHUNK, BLOCK), 1) - REACH
             row_weight = lanczos(row_shift - row_step.astype(jnp.float32))
-            col_shift = affine_ref[place * 4 + 2] + affine_ref[place * 4 + 3] * (
+            col_shift = affine_ref[visit, ccd, 1, 0] + affine_ref[visit, ccd, 1, 1] * (
                 (column - (WIDTH - 1) / 2.0) / WIDTH
             )
             col_step = lax.broadcasted_iota(jnp.int32, (8, WIDTH), 0) - REACH
@@ -324,7 +330,6 @@
     patch = jnp.int32(0)
     for candidate in range(owner_ref.shape[0]):
         patch = jnp.where(owner_ref[candidate] == me, candidate, patch)
-    ccds = weight_ref.shape[0] // V
     count = V * BLKC
 
     def add(source, carry):
@@ -336,7 +341,7 @@
             @pl.when(mine)
             def _(taken=taken, block=block):
                 cell = meta_ref[source, 0, count + block]
-                weight = weight_ref[block // BLKC * ccds + ccd]
+                weight = weight_ref[block // BLKC, ccd]
                 weights[cell] = weights[cell] + weight
                 for chunk in range(CHUNKS):
                     rows = pl.ds(chunk * CHUNK, CHUNK)
@@ -365,9 +370,6 @@
     scalars = pl.BlockSpec(memory_space=pltpu.SMEM)
     vector = pl.BlockSpec(memory_space=pltpu.VMEM)
     lanes = -(-2 * block_count // BLOCK) * BLOCK
-    meta = jnp.pad(
-        jnp.concatenate([block_patch[0, :, 0], block_slot[0]]), (0, lanes - 2 * block_count)
-    )[None]
     rim_shape = jax.ShapeDtypeStruct((V, RIM, WIDTH), jnp.float32)
     above, below = pl.pallas_call(
         functools.partial(rim_kernel, devices),
@@ -378,13 +380,16 @@
         compiler_params=pltpu.CompilerParams(collective_id=1, has_side_effects=True),
     )(images)
 
-    blocks = pl.pallas_call(
+    blocks, meta = pl.pallas_call(
         functools.partial(plan_kernel, devices, capacity),
-        out_shape=jax.ShapeDtypeStruct((slots,), jnp.int32),
-        in_specs=[scalars, scalars],
-        out_specs=scalars,
+        out_shape=(
+            jax.ShapeDtypeStruct((slots,), jnp.int32),
+            jax.ShapeDtypeStruct((1, lanes), jnp.int32),
+        ),
+        in_specs=[scalars] * 3,
+        out_specs=(scalars, vector),
         scratch_shapes=[pltpu.SMEM((devices,), jnp.int32)],
-    )(block_patch.reshape(-1), patch_owner)
+    )(block_patch.reshape(-1), block_slot, patch_owner)
     metas, got = pl.pallas_call(
         functools.partial(band_kernel, devices, capacity),
         out_shape=(
@@ -410,9 +415,9 @@
         compiler_params=pltpu.CompilerParams(collective_id=2, has_side_effects=True),
     )(
         blocks,
-        basis_taps.reshape(-1),
+        basis_taps,
         psf_coef.reshape(-1),
-        affine.reshape(-1),
+        affine,
         meta,
         above,
         images,
@@ -428,7 +433,7 @@
             pltpu.VMEM((PSIDE * PSIDE, BLOCK, BLOCK), jnp.float32),
             pltpu.SMEM((PSIDE * PSIDE,), jnp.float32),
         ],
-    )(metas, patch_owner, visit_weight.astype(jnp.float32).reshape(-1), got.reshape(CHUNKS, slots, CHUNK, BLOCK))
+    )(metas, patch_owner, visit_weight.astype(jnp.float32), got.reshape(CHUNKS, slots, CHUNK, BLOCK))
 
 
 def solution(mesh):

time: 56.8 us -> 55.8 us (0.982)
  local copies, waits for them, and re-layouts: 4.46 us -> 2.47 us
    reshape x3 -> x0, local copies, waits for them, and re-layouts: 2.7 us -> none  [the longest x1 1.37 us: shards(): visit_weight.astype(jnp.float32).reshape(-1)]
    unnamed x9, local copies, waits for them, and re-layouts: 0.39 us -> 1.68 us
    convert_element_type x0 -> x1, other arithmetic: none -> 1.26 us  [shards(): visit_weight.astype(jnp.float32)]
    concatenate x1 -> x0, other arithmetic: 0.75 us -> none  [shards(): jnp.concatenate([block_patch[0, :, 0], block_slot[0]])]
    broadcast_in_dim x1 -> x0, local copies, waits for them, and re-layouts: 0.58 us -> none  [shards(): jnp.pad(jnp.concatenate([block_patch[0, :, 0], block_slot[0]]), (0, lanes...]
where the time goes in v5:
time: 55.8 us; the launch traced here: 55.4 us
  Pallas kernels  51.6 us (92%)
  local copies, waits for them, and re-layouts  2.47 us (4%)
  other arithmetic  1.26 us (2%)
    pallas_call x1, Pallas kernels, shards(): pl.pallas_call(functools.partial(band_kernel, devices, capacity), out_sha...  40.9 us
    pallas_call x1, Pallas kernels, shards(): pl.pallas_call(functools.partial(gather_kernel, devices, capacity), out_s...  5.06 us
    pallas_call x1, Pallas kernels, shards(): pl.pallas_call(functools.partial(rim_kernel, devices), out_shape=(rim_sha...  4.23 us
    unnamed x9, local copies, waits for them, and re-layouts  1.68 us
    pallas_call x1, Pallas kernels, shards(): pl.pallas_call(functools.partial(plan_kernel, devices, capacity), out_sha...  1.44 us
    convert_element_type x1, other arithmetic, shards(): visit_weight.astype(jnp.float32)  1.26 us

profile of v5, /device:TPU:0, one launch (start us, length us, event | category | flops | bytes accessed | tf_op | source)
XLA Modules:
  0.0 55.4 jit_solution(15631976017425419716)
XLA Ops:
  0.0 0.0 copy-start.1
  0.0 1.4 %shard_map.82 = (s32[32]{0:T(128)}, s32[1,128]{1,0:T(1,128)}) custom-call(s32[16]{0:T(128)} %bitcast.3, s32[1,16]{1,0:T(1,128)} %slot_ref.1, s32[16]{0:T(128)} %owner_ref.3), custom_call_target="tpu_custom_call" | custom-call | tf_op jit(solution)/shard_map/pallas_call | solution.py:383
  1.4 1.3 %convert_element_type.3.weight_ref = f32[4,5]{1,0:T(4,128)} convert(bf16[4,5]{1,0:T(4,128)(2,1)} %param.12) | non-fusion elementwise | flops 20 | bytes 120 | tf_op jit(solution)/shard_map/convert_element_type | solution.py:436
  2.7 0.0 copy-done.1
  2.7 0.0 copy-start.2
  2.7 0.6 %copy.12.taps_ref = f32[2,9,11]{2,1,0:T(8,128)} copy(f32[2,9,11]{2,0,1:T(2,128)S(1)} %copy-done.1) | data formatting | bytes 1584 | tf_op args[1]
  3.3 0.1 copy-done.2
  3.4 0.7 %copy.13.affine_ref = f32[4,5,2,2]{3,2,1,0:T(2,128)} copy(f32[4,5,2,2]{1,3,2,0:T(2,128)S(1)} %copy-done.2) | data formatting | bytes 640 | tf_op args[3]
  4.2 0.0 copy-start
  4.2 4.2 %shard_map.83 = (f32[4,8,512]{2,1,0:T(8,128)}, f32[4,8,512]{2,1,0:T(8,128)}) custom-call(f32[4,128,512]{2,1,0:T(8,128)} %image_ref.3), custom_call_target="tpu_custom_call" | custom-call | tf_op jit(solution)/shard_map/pallas_call | solution.py:374
  8.4 0.0 copy-done
  8.4 0.2 copy.11
  8.6 0.8 %reshape.10.coef_ref = f32[540]{0:T(1024)} reshape(f32[4,5,9,3]{3,2,1,0:T(8,128)S(1)} %copy.11) | data formatting | bytes 4320 | tf_op jit(solution)/shard_map/reshape | solution.py:419
  9.4 40.9 %shard_map.84 = (s32[16,1,128]{2,1,0:T(1,128)}, bf16[2,16,2,64,128]{4,3,2,1,0:T(8,128)(2,1)}) custom-call(s32[32]{0:T(128)} %get-tuple-element.11.block_ref, f32[2,9,11]{2,1,0:T(8,128)} %copy.12.taps_ref, f32[540]{0:T(1024)} %reshape.10.coef_ref, f32[4,5,2,2]{3,2,1,0:T(2,128)} %copy.13.affine_ref, s32[1,128]{1,0:T(1,128)} %get-tuple-element.12.meta_ref, ...), custom_call_target="tpu_custom_call" | custom-call | tf_op jit(solution)/shard_map/pallas_call | solution.py:393
  50.3 5.1 %shard_map.85 = f32[1,512,512]{2,1,0:T(8,128)} custom-call(s32[16,1,128]{2,1,0:T(1,128)} %get-tuple-element.15.meta_ref, s32[16]{0:T(128)} %owner_ref.3, f32[4,5]{1,0:T(4,128)} %convert_element_type.3.weight_ref, bf16[2,32,64,128]{3,2,1,0:T(8,128)(2,1)} %bitcast.2), custom_call_target="tpu_custom_call" | custom-call | tf_op jit(solution)/shard_map/pallas_call | solution.py:427
Async XLA Ops:
  0.0 2.7 %copy-start.1 = (f32[2,9,11]{2,0,1:T(2,128)S(1)}, f32[2,9,11]{2,0,1:T(2,128)}, u32[]{:S(2)}) copy-start(f32[2,9,11]{2,0,1:T(2,128)} %param.9) | copy-start | bytes 2380
  2.7 0.7 %copy-start.2 = (f32[4,5,2,2]{1,3,2,0:T(2,128)S(1)}, f32[4,5,2,2]{1,3,2,0:T(2,128)}, u32[]{:S(2)}) copy-start(f32[4,5,2,2]{1,3,2,0:T(2,128)} %param.11) | copy-start | bytes 964
  4.2 4.2 %copy-start = (f32[4,5,9,3]{2,0,3,1:T(4,128)S(1)}, f32[4,5,9,3]{2,0,3,1:T(4,128)}, u32[]{:S(2)}) copy-start(f32[4,5,9,3]{2,0,3,1:T(4,128)} %param.10) | copy-start | bytes 6484

commit v6 on v5

--- a/solution.py
+++ b/solution.py
@@ -39,7 +39,11 @@
 
 
 def outward(count):
-    return sorted(range(1, count), key=lambda step: abs(step - count // 2))
+    far = sorted(range(1, count), key=lambda step: abs(step - count // 2))
+    half = len(far) // 2
+    near = far[half:][::-1]
+    mixed = [step for pair in zip(far[:half], near) for step in pair]
+    return mixed + near[half:]
 
 
 def rim_kernel(count, image_ref, above_ref, below_ref, rims):

time: 55.8 us -> 55.7 us (level)
  no operation moved by 1% of the time
where the time goes in v6:
time: 55.7 us; the launch traced here: 55.4 us
  Pallas kernels  51.6 us (93%)
  local copies, waits for them, and re-layouts  2.47 us (4%)
  other arithmetic  1.26 us (2%)
    pallas_call x1, Pallas kernels, shards(): pl.pallas_call(functools.partial(band_kernel, devices, capacity), out_sha...  40.9 us
    pallas_call x1, Pallas kernels, shards(): pl.pallas_call(functools.partial(gather_kernel, devices, capacity), out_s...  5.06 us
    pallas_call x1, Pallas kernels, shards(): pl.pallas_call(functools.partial(rim_kernel, devices), out_shape=(rim_sha...  4.23 us
    unnamed x9, local copies, waits for them, and re-layouts  1.68 us
    pallas_call x1, Pallas kernels, shards(): pl.pallas_call(functools.partial(plan_kernel, devices, capacity), out_sha...  1.44 us
    convert_element_type x1, other arithmetic, shards(): visit_weight.astype(jnp.float32)  1.26 us

profile of v6, /device:TPU:0, one launch (start us, length us, event | category | flops | bytes accessed | tf_op | source)
XLA Modules:
  0.0 55.4 jit_solution(11422513502979667823)
XLA Ops:
  0.0 0.0 copy-start.1
  0.0 1.4 %shard_map.82 = (s32[32]{0:T(128)}, s32[1,128]{1,0:T(1,128)}) custom-call(s32[16]{0:T(128)} %bitcast.3, s32[1,16]{1,0:T(1,128)} %slot_ref.1, s32[16]{0:T(128)} %owner_ref.3), custom_call_target="tpu_custom_call" | custom-call | tf_op jit(solution)/shard_map/pallas_call | solution.py:387
  1.4 1.3 %convert_element_type.3.weight_ref = f32[4,5]{1,0:T(4,128)} convert(bf16[4,5]{1,0:T(4,128)(2,1)} %param.12) | non-fusion elementwise | flops 20 | bytes 120 | tf_op jit(solution)/shard_map/convert_element_type | solution.py:440
  2.7 0.0 copy-done.1
  2.7 0.0 copy-start.2
  2.7 0.6 %copy.12.taps_ref = f32[2,9,11]{2,1,0:T(8,128)} copy(f32[2,9,11]{2,0,1:T(2,128)S(1)} %copy-done.1) | data formatting | bytes 1584 | tf_op args[1]
  3.3 0.1 copy-done.2
  3.4 0.7 %copy.13.affine_ref = f32[4,5,2,2]{3,2,1,0:T(2,128)} copy(f32[4,5,2,2]{1,3,2,0:T(2,128)S(1)} %copy-done.2) | data formatting | bytes 640 | tf_op args[3]
  4.2 0.0 copy-start
  4.2 4.2 %shard_map.83 = (f32[4,8,512]{2,1,0:T(8,128)}, f32[4,8,512]{2,1,0:T(8,128)}) custom-call(f32[4,128,512]{2,1,0:T(8,128)} %image_ref.3), custom_call_target="tpu_custom_call" | custom-call | tf_op jit(solution)/shard_map/pallas_call | solution.py:378
  8.4 0.0 copy-done
  8.4 0.2 copy.11
  8.6 0.8 %reshape.10.coef_ref = f32[540]{0:T(1024)} reshape(f32[4,5,9,3]{3,2,1,0:T(8,128)S(1)} %copy.11) | data formatting | bytes 4320 | tf_op jit(solution)/shard_map/reshape | solution.py:423
  9.4 40.9 %shard_map.84 = (s32[16,1,128]{2,1,0:T(1,128)}, bf16[2,16,2,64,128]{4,3,2,1,0:T(8,128)(2,1)}) custom-call(s32[32]{0:T(128)} %get-tuple-element.11.block_ref, f32[2,9,11]{2,1,0:T(8,128)} %copy.12.taps_ref, f32[540]{0:T(1024)} %reshape.10.coef_ref, f32[4,5,2,2]{3,2,1,0:T(2,128)} %copy.13.affine_ref, s32[1,128]{1,0:T(1,128)} %get-tuple-element.12.meta_ref, ...), custom_call_target="tpu_custom_call" | custom-call | tf_op jit(solution)/shard_map/pallas_call | solution.py:397
  50.3 5.1 %shard_map.85 = f32[1,512,512]{2,1,0:T(8,128)} custom-call(s32[16,1,128]{2,1,0:T(1,128)} %get-tuple-element.15.meta_ref, s32[16]{0:T(128)} %owner_ref.3, f32[4,5]{1,0:T(4,128)} %convert_element_type.3.weight_ref, bf16[2,32,64,128]{3,2,1,0:T(8,128)(2,1)} %bitcast.2), custom_call_target="tpu_custom_call" | custom-call | tf_op jit(solution)/shard_map/pallas_call | solution.py:431
Async XLA Ops:
  0.0 2.7 %copy-start.1 = (f32[2,9,11]{2,0,1:T(2,128)S(1)}, f32[2,9,11]{2,0,1:T(2,128)}, u32[]{:S(2)}) copy-start(f32[2,9,11]{2,0,1:T(2,128)} %param.9) | copy-start | bytes 2380
  2.7 0.7 %copy-start.2 = (f32[4,5,2,2]{1,3,2,0:T(2,128)S(1)}, f32[4,5,2,2]{1,3,2,0:T(2,128)}, u32[]{:S(2)}) copy-start(f32[4,5,2,2]{1,3,2,0:T(2,128)} %param.11) | copy-start | bytes 964
  4.2 4.2 %copy-start = (f32[4,5,9,3]{2,0,3,1:T(4,128)S(1)}, f32[4,5,9,3]{2,0,3,1:T(4,128)}, u32[]{:S(2)}) copy-start(f32[4,5,9,3]{2,0,3,1:T(4,128)} %param.10) | copy-start | bytes 6484
